TPU v7x, 256 devices: a whole 4x4x8 slice. The times are simulated.
256 devices in a mesh: ctx: 32 (over x_lo, z, core), exp: 8 (over x_hi, y).
Axes of the slice: x: 4 (x_hi: 2, x_lo: 2; x = x_hi * 2 + x_lo), y: 4, z: 8, core: 2. Of those that a mesh axis runs over, the one named last changes fastest.
Arguments:
- queries: bfloat16 [8192, 8192], P('ctx', 'exp'), may hold values from -8 to 8
- keys: bfloat16 [8192, 512], P('ctx'), may hold values from -4 to 4
- values: bfloat16 [8192, 512], P('ctx'), may hold values from -6 to 6
- w_out: bfloat16 [8192, 4096], P('exp'), may hold values from -0.5 to 0.5
- residual: bfloat16 [8192, 4096], P(('ctx', 'exp')), may hold values from -1.5 to 1.5
- norm_gain: bfloat16 [4096], replicated, may hold values from 0.099609375 to 1.8984375
- expert_ids: int32 [8192, 2], P(('ctx', 'exp')), may hold values from 0 to 7, all different within a row; in each aligned block of 32 rows (0 to 31, 32 to 63, ...) at most 16 rows name the same one
- gate_weights: float32 [8192, 2], P(('ctx', 'exp')), may hold values from 0.2 to 1
- w_gate: bfloat16 [8, 4096, 768], P('exp', 'ctx'), may hold values from -0.09375 to 0.09375
- w_up: bfloat16 [8, 4096, 768], P('exp', 'ctx'), may hold values from -0.09375 to 0.09375
- w_down: bfloat16 [8, 768, 4096], P('exp', None, 'ctx'), may hold values from -0.21875 to 0.21875
Outputs:
- layer_out: bfloat16 [8192, 4096], P(('ctx', 'exp'))
Inputs may be any that keep to these rules, and one draw needn't show every extreme that they name: `expert_ids`: each row names 2 different experts; within each aligned block of 32 rows (the rows of one device) no expert is named by more than 16 rows.
All inputs are finite; a program needn't handle non-finite values.
Results may differ from a plain program's by a relative error of at most 0.025.
Values may be sent and summed in bfloat16 or wider, within the bound.
A program may use at most 128 MiB of HBM per device.

v0:
```python
import math

import jax
import jax.numpy as jnp
from jax import lax
from jax.sharding import PartitionSpec as P

D = 4096
HQ = 64
KVH = 4
HD = 128


def body(
    queries,
    keys,
    values,
    w_out,
    residual,
    norm_gain,
    expert_ids,
    gate_weights,
    w_gate,
    w_up,
    w_down,
):
    tok_rows = queries.shape[0]
    half_rows = tok_rows // 2
    exp_count = lax.axis_size("exp")
    heads_here = HQ // exp_count
    group = HQ // KVH
    kv_here = max(1, heads_here // group)
    heads_per_kv = heads_here // kv_here
    exp_index = lax.axis_index("exp")
    ctx_index = lax.axis_index("ctx")
    kv_first = exp_index * heads_here // group
    key_cols = lax.dynamic_slice_in_dim(keys, kv_first * HD, kv_here * HD, 1)
    value_cols = lax.dynamic_slice_in_dim(values, kv_first * HD, kv_here * HD, 1)
    scale = 1.0 / math.sqrt(HD)
    first_rows = queries[:half_rows]
    second_rows = queries[half_rows:]
    first_start = ctx_index * tok_rows
    second_start = ctx_index * tok_rows + half_rows
    query_sets = (
        first_rows.reshape(half_rows, kv_here, heads_per_kv, HD),
        second_rows.reshape(half_rows, kv_here, heads_per_kv, HD),
    )
    query_positions = (
        first_start + jnp.arange(half_rows, dtype=jnp.int32),
        second_start + jnp.arange(half_rows, dtype=jnp.int32),
    )
    last_positions = (first_start + half_rows - 1, second_start + half_rows - 1)

    def block_update(carry, query_four, query_pos, key_block, value_block, key_start):
        run_max, run_sum, run_acc = carry
        width = key_block.shape[0]
        key_three = key_block.reshape(width, kv_here, HD)
        value_three = value_block.reshape(width, kv_here, HD)
        scores = (
            jnp.einsum("tghd,kgd->ghtk", query_four, key_three, preferred_element_type=jnp.float32)
            * scale
        )
        key_pos = key_start + jnp.arange(width, dtype=jnp.int32)
        allowed = key_pos[None, :] <= query_pos[:, None]
        scores = jnp.where(allowed, scores, -1e30)
        new_max = jnp.maximum(run_max, jnp.max(scores, axis=-1))
        probs = jnp.where(allowed, jnp.exp(scores - new_max[..., None]), 0.0)
        factor = jnp.exp(run_max - new_max)
        run_sum = run_sum * factor + jnp.sum(probs, axis=-1)
        weighted = jnp.einsum(
            "ghtk,kgd->ghtd",
            probs.astype(jnp.bfloat16),
            value_three,
            preferred_element_type=jnp.float32,
        )
        run_acc = run_acc * factor[..., None] + weighted
        return (new_max, run_sum, run_acc)

    start_max = jnp.full((kv_here, heads_per_kv, half_rows), -1e30, jnp.float32)
    start_sum = jnp.zeros((kv_here, heads_per_kv, half_rows), jnp.float32)
    start_acc = jnp.zeros((kv_here, heads_per_kv, half_rows, HD), jnp.float32)
    start_state = (start_max, start_sum, start_acc)
    key_piece = lax.all_gather(key_cols, "ctx", axis=0, tiled=True)
    value_piece = lax.all_gather(value_cols, "ctx", axis=0, tiled=True)
    count = key_piece.shape[0]
    width = 512

    def one_block(index, inner):
        key_start = index * width
        key_block = lax.dynamic_slice_in_dim(key_piece, key_start, width, 0)
        value_block = lax.dynamic_slice_in_dim(value_piece, key_start, width, 0)
        updated = []
        for which in range(2):
            query_four = query_sets[which]
            query_pos = query_positions[which]
            updated.append(
                lax.cond(
                    key_start > last_positions[which],
                    lambda state: state,
                    lambda state: block_update(
                        state, query_four, query_pos, key_block, value_block, key_start
                    ),
                    inner[which],
                )
            )
        return (updated[0], updated[1])

    states = lax.fori_loop(0, count // width, one_block, (start_state, start_state))
    halves = []
    for which in range(2):
        run_max, run_sum, run_acc = states[which]
        halves.append(
            jnp.transpose(run_acc / run_sum[..., None], (2, 0, 1, 3))
            .reshape(half_rows, heads_here * HD)
            .astype(jnp.bfloat16)
        )
    attn_second = halves[1]
    attn = jnp.concatenate([halves[0], attn_second], axis=0)
    projected = lax.psum_scatter(
        jnp.dot(attn, w_out, preferred_element_type=jnp.float32).astype(jnp.bfloat16),
        "exp",
        scatter_dimension=0,
        tiled=True,
    ).astype(jnp.float32)
    hidden_state = (residual.astype(jnp.float32) + projected).astype(jnp.bfloat16)
    state_f = hidden_state.astype(jnp.float32)
    inv_rms = 1.0 / jnp.sqrt(jnp.mean(state_f * state_f, axis=1, keepdims=True) + 1e-06)
    normed = (state_f * inv_rms * norm_gain.astype(jnp.float32)[None, :]).astype(jnp.bfloat16)
    rows_here = expert_ids.shape[0]
    top_count = expert_ids.shape[1]
    experts_all = w_gate.shape[0] * exp_count
    capacity = min(rows_here, 2 * rows_here * top_count // experts_all)
    flat_ids = expert_ids.reshape(-1)
    onehot = (flat_ids[:, None] == jnp.arange(experts_all, dtype=jnp.int32)[None, :]).astype(
        jnp.int32
    )
    earlier = jnp.cumsum(onehot, axis=0) - onehot
    slot_index = jnp.sum(earlier * onehot, axis=1)
    target = flat_ids * capacity + slot_index
    picks = target[:, None] == jnp.arange(experts_all * capacity, dtype=jnp.int32)[None, :]
    dispatch_table = jnp.any(
        picks.reshape(rows_here, top_count, experts_all * capacity), axis=1
    ).astype(jnp.bfloat16)
    outgoing = jnp.einsum(
        "rs,rd->sd", dispatch_table, normed, preferred_element_type=jnp.float32
    ).astype(jnp.bfloat16)
    arrived = lax.all_to_all(
        outgoing.reshape(experts_all, capacity, D), "exp", split_axis=0, concat_axis=0, tiled=True
    )
    slot_rows = arrived.reshape(experts_all * capacity, D)
    gate_local = w_gate[0]
    up_local = w_up[0]
    gate_pre = jnp.dot(
        slot_rows,
        lax.all_gather(gate_local, "ctx", axis=0, tiled=True),
        preferred_element_type=jnp.float32,
    )
    up_pre = jnp.dot(
        slot_rows,
        lax.all_gather(up_local, "ctx", axis=0, tiled=True),
        preferred_element_type=jnp.float32,
    )
    expert_hidden = (jax.nn.silu(gate_pre) * up_pre).astype(jnp.bfloat16)
    down_local = w_down[0]
    expert_result = jnp.dot(
        expert_hidden,
        lax.all_gather(down_local, "ctx", axis=1, tiled=True),
        preferred_element_type=jnp.float32,
    ).astype(jnp.bfloat16)
    returned = lax.all_to_all(
        expert_result.reshape(experts_all, capacity, D),
        "exp",
        split_axis=0,
        concat_axis=0,
        tiled=True,
    )
    returned_flat = returned.reshape(experts_all * capacity, D)
    picked = jnp.dot(picks.astype(jnp.bfloat16), returned_flat, preferred_element_type=jnp.float32)
    weighted = gate_weights[:, :, None] * picked.reshape(rows_here, top_count, D)
    return (state_f + jnp.sum(weighted, axis=1)).astype(jnp.bfloat16)


def solution(mesh):
    placed = (
        P("ctx", "exp"),
        P("ctx", None),
        P("ctx", None),
        P("exp", None),
        P(("ctx", "exp"), None),
        P(),
        P(("ctx", "exp"), None),
        P(("ctx", "exp"), None),
        P("exp", "ctx", None),
        P("exp", "ctx", None),
        P("exp", None, "ctx"),
    )
    return jax.shard_map(
        body, mesh=mesh, in_specs=placed, out_specs=P(("ctx", "exp"), None), check_vma=False
    )
```

profile of v0, /device:TPU:1, one launch (start us, length us, event | category | flops | bytes accessed | tf_op | source)
XLA Modules:
  0.0 572.9 jit_solution(10112256670926563452)
XLA Ops:
  8.2 1.5 constant_dynamic-slice_fusion.3
  9.7 1.1 fusion.83
  11.5 66.6 %all-gather.11.cloned.1.call-done = bf16[8192,128]{1,0:T(8,128)(2,1)} async-done(((bf16[256,128]{1,0:T(8,128)(2,1)}), bf16[8192,128]{1,0:T(8,128)(2,1)}) %all-gather.11.cloned.1.call-update) | async-done | bytes 2097168 | tf_op jit(solution)/shard_map/all_gather | solution.py:84
  78.1 66.3 %all-gather.9.cloned.1.call-done = bf16[8192,128]{1,0:T(8,128)(2,1)} async-done(((bf16[256,128]{1,0:T(8,128)(2,1)}), bf16[8192,128]{1,0:T(8,128)(2,1)}) %all-gather.9.cloned.1.call-update) | async-done | bytes 2097168 | tf_op jit(solution)/shard_map/all_gather | solution.py:83
  144.5 22.4 %while.24 = (s32[]{:T(128)}, f32[1,8,128]{2,1,0:T(8,128)S(1)}, f32[1,8,128]{2,1,0:T(8,128)S(1)}, f32[1,8,128,128]{3,2,1,0:T(8,128)S(1)}, f32[1,8,128]{2,1,0:T(8,...) while((s32[]{:T(128)}, f32[1,8,128]{2,1,0:T(8,128)S(1)}, ...), condition=%wide.region_9.10_spmd.clone, body=%wide.region_0.9_spmd.clone.sunk | while | flops 551165184 | bytes 16921084 | solution.py:108
  144.6 1.0 constant_dynamic-slice_fusion.5
  145.6 2.0 conditional.7
  147.6 2.0 conditional.6
  149.7 1.0 constant_dynamic-slice_fusion.5
  150.9 1.0 constant_dynamic-slice_fusion.5
  152.0 1.0 constant_dynamic-slice_fusion.5
  153.2 1.0 constant_dynamic-slice_fusion.5
  154.3 1.0 constant_dynamic-slice_fusion.5
  155.5 1.0 constant_dynamic-slice_fusion.5
  156.6 1.0 constant_dynamic-slice_fusion.5
  157.7 1.0 constant_dynamic-slice_fusion.5
  158.9 1.0 constant_dynamic-slice_fusion.5
  160.0 1.0 constant_dynamic-slice_fusion.5
  161.2 1.0 constant_dynamic-slice_fusion.5
  162.3 1.0 constant_dynamic-slice_fusion.5
  163.5 1.0 constant_dynamic-slice_fusion.5
  167.4 7.1 %convolution_convert_fusion = bf16[256,4096]{1,0:T(8,128)(2,1)} fusion(bf16[1024,4096]{1,0:T(8,128)(2,1)} %param.20, bf16[128,1024]{0,1:T(8,128)(2,1)S(1)} %bitcast.139, bf16[128,1024]{0,1:T(8,128)(2,1)S(1)} %bitcast.138), kind=kOutput, calls=%fused_computation.64 | convolution fusion | flops 2149580800 | bytes 11010048 | tf_op jit(solution)/shard_map/dot_general | solution.py:120
  177.1 132.3 %reduce-scatter.2.cloned.1.call-done = bf16[32,4096]{1,0:T(8,128)(2,1)} async-done(((bf16[256,4096]{1,0:T(8,128)(2,1)}), bf16[32,4096]{1,0:T(8,128)(2,1)}) %reduce-scatter.2.cloned.1.call-update) | async-done | bytes 262160 | tf_op jit(solution)/shard_map/reduce_scatter | solution.py:119
  309.5 1.1 fusion.60
  310.6 1.5 convolution_convert_fusion.1
  312.1 18.5 %all_to_all.10 = bf16[8,16,4096]{2,1,0:T(8,128)(2,1)S(1)} all-to-all(bf16[8,16,4096]{2,1,0:T(8,128)(2,1)S(1)} %bitcast.130), channel_id=1, replica_groups=mesh['ctx'=32,'exp'=8] {'exp'}, dimensions={0} | all-to-all | bytes 2097152 | tf_op jit(solution)/shard_map/all_to_all | solution.py:147
  330.6 51.6 %all-gather.13.cloned.1.call-done = bf16[1,4096,768]{2,1,0:T(8,128)(2,1)} async-done(((bf16[1,128,768]{2,1,0:T(8,128)(2,1)}), bf16[1,4096,768]{2,1,0:T(8,128)(2,1)}) %all-gather.13.cloned.1.call-update) | async-done | bytes 6291472 | tf_op jit(solution)/shard_map/all_gather | solution.py:155
  382.2 3.8 fusion.46
  386.0 67.8 %all-gather.15.cloned.1.call-done = bf16[1,4096,768]{2,1,0:T(8,128)(2,1)} async-done(((bf16[1,128,768]{2,1,0:T(8,128)(2,1)}), bf16[1,4096,768]{2,1,0:T(8,128)(2,1)}) %all-gather.15.cloned.1.call-update) | async-done | bytes 6291472 | tf_op jit(solution)/shard_map/all_gather | solution.py:160
  453.7 82.0 %all-gather.17.cloned.1.call-done = bf16[1,768,4096]{2,1,0:T(8,128)(2,1)} async-done(((bf16[1,768,128]{2,1,0:T(8,128)(2,1)}), bf16[1,768,4096]{2,1,0:T(8,128)(2,1)}) %all-gather.17.cloned.1.call-update) | async-done | bytes 6291472 | tf_op jit(solution)/shard_map/all_gather | solution.py:167
  535.7 7.1 %fusion.48 = bf16[128,4096]{1,0:T(8,128)(2,1)S(1)} fusion(bf16[1,768,4096]{2,1,0:T(8,128)(2,1)} %all-gather.17.cloned.1.call-done, bf16[128,4096]{1,0:T(8,128)(2,1)S(1)} %bitcast.128, bf16[1,4096,768]{2,1,0:T(8,128)(2,1)} %all-gather.15.cloned.1.call-done, f32[128,768]{1,0:T(8,128)S(1)} %fusion.46), kind=kOutput, calls=%fused_computation.65 | convolution fusion | flops 1611726848 | bytes 15073280 | tf_op jit(solution)/shard_map/dot_general | solution.py:165
  542.8 22.1 %all_to_all.11 = bf16[8,16,4096]{2,1,0:T(8,128)(2,1)S(1)} all-to-all(bf16[8,16,4096]{2,1,0:T(8,128)(2,1)S(1)} %bitcast.129), channel_id=1, replica_groups=mesh['ctx'=32,'exp'=8] {'exp'}, dimensions={0} | all-to-all | bytes 2097152 | tf_op jit(solution)/shard_map/all_to_all | solution.py:170
  (194 shorter events, 13.7 us)
Async XLA Ops:
  6.5 1.0 copy-start
  6.5 71.6 %all-gather.11.cloned.1.call-start = ((), (), s32[]{:S(2)}) async-start(), calls=%async_computation.4 | async-start | bytes 2162688 | tf_op jit(solution)/shard_map/all_gather | solution.py:84
  8.1 136.3 %all-gather.9.cloned.1.call-start = ((), (), s32[]{:S(2)}) async-start(), calls=%async_computation.3 | async-start | bytes 2162688 | tf_op jit(solution)/shard_map/all_gather | solution.py:83
  9.7 299.8 %reduce-scatter.2.cloned.1.call-start = ((), (), s32[]{:S(2)}) async-start(), calls=%async_computation.5 | async-start | bytes 2359296 | tf_op jit(solution)/shard_map/reduce_scatter | solution.py:119
  174.5 1.8 copy-start.4
  174.5 2.5 copy-start.3
  174.5 135.0 %copy-start.1 = (bf16[32,4096]{1,0:T(8,128)(2,1)S(1)}, bf16[32,4096]{1,0:T(8,128)(2,1)}, u32[]{:S(2)}) copy-start(bf16[32,4096]{1,0:T(8,128)(2,1)} %param.21) | copy-start | bytes 786436
  174.5 207.6 %all-gather.13.cloned.1.call-start = ((), (), s32[]{:S(2)}) async-start(), calls=%async_computation.6 | async-start | bytes 6488064 | tf_op jit(solution)/shard_map/all_gather | solution.py:155
  175.1 278.6 %all-gather.15.cloned.1.call-start = ((), (), s32[]{:S(2)}) async-start(), calls=%async_computation.7 | async-start | bytes 6488064 | tf_op jit(solution)/shard_map/all_gather | solution.py:160
  175.7 360.0 %all-gather.17.cloned.1.call-start = ((), (), s32[]{:S(2)}) async-start(), calls=%async_computation.8 | async-start | bytes 6488064 | tf_op jit(solution)/shard_map/all_gather | solution.py:167
  542.8 22.1 %copy-start.5 = (f32[32,2]{0,1:T(2,128)S(1)}, f32[32,2]{0,1:T(2,128)}, u32[]{:S(2)}) copy-start(f32[32,2]{0,1:T(2,128)} %param.24) | copy-start | bytes 772
  542.8 22.5 %copy-start.2 = (bf16[32,4096]{1,0:T(8,128)(2,1)S(1)}, bf16[32,4096]{1,0:T(8,128)(2,1)}, u32[]{:S(2)}) copy-start(bf16[32,4096]{1,0:T(8,128)(2,1)} %reduce-scatter.2.cloned.1.call-done) | copy-start | bytes 786436
Sparse Core Ops, SparseCore 0:
  9.2 68.8 all-gather.10
  80.0 64.3 all-gather.8
  174.7 134.7 reduce-scatter.1
  311.2 70.9 all-gather.12
  383.9 69.8 all-gather.14
  455.4 80.3 all-gather.16
where the time goes:
time: 574 us; the launch traced here: 573 us
  waiting for transfers between devices  468 us (82%)
  blocking collectives  40.6 us (7%)
  matrix products  22.3 us (4%)
  local copies, waits for them, and re-layouts  21.8 us (4%)
  between operations  13.7 us (2%)
    reduce_scatter x1, waiting for transfers between devices, body(): lax.psum_scatter(jnp.dot(attn, w_out, preferred_element_type=jnp.float32)...  132 us
    all_gather x1, waiting for transfers between devices, body(): lax.all_gather(down_local, 'ctx', axis=1, tiled=True)  82 us
    all_gather x1, waiting for transfers between devices, body(): lax.all_gather(up_local, 'ctx', axis=0, tiled=True)  67.8 us
    all_gather x1, waiting for transfers between devices, body(): value_piece = lax.all_gather(value_cols, 'ctx', axis=0, tiled=True)  66.6 us
    all_gather x1, waiting for transfers between devices, body(): key_piece = lax.all_gather(key_cols, 'ctx', axis=0, tiled=True)  66.3 us
    all_gather x1, waiting for transfers between devices, body(): lax.all_gather(gate_local, 'ctx', axis=0, tiled=True)  51.6 us
    all_to_all x1, blocking collectives, body(): lax.all_to_all(expert_result.reshape(experts_all, capacity, D), 'exp', sp...  22.1 us
    all_to_all x1, blocking collectives, body(): lax.all_to_all(outgoing.reshape(experts_all, capacity, D), 'exp', split_a...  18.5 us
  transfers between devices with their start and end apart: 6, of which 6 were waited for; matrix products, arithmetic and copies ran while one was open for 2% of the time, Pallas kernels for 0%

commit v1 on v0

v1 whole, which is shorter than its diff:
```python
import functools
import math

import jax
import jax.numpy as jnp
from jax import lax
from jax.experimental import pallas as pl
from jax.experimental.pallas import tpu as pltpu
from jax.sharding import PartitionSpec as P

D = 4096
HQ = 64
KVH = 4
HD = 128
FF = 768
EXPERTS = 8
CAP = 16
ROWS = 32
NX, NZ, NC = 2, 8, 2
CTX = NX * NZ * NC
EXP = 8
TOK = 256
HALF = 128
HEADS = HQ // EXP
MESH = pl.DeviceIdType.MESH
MIB = 1 << 20
F32 = jnp.float32
BF16 = jnp.bfloat16


def remote(src, dst, send, recv, ctx, exp):
    return pltpu.make_async_remote_copy(
        src_ref=src, dst_ref=dst, send_sem=send, recv_sem=recv, device_id=(ctx, exp), device_id_type=MESH
    )


def greet(peers):
    barrier = pltpu.get_barrier_semaphore()
    for ctx, exp in peers:
        pl.semaphore_signal(barrier, inc=1, device_id=(ctx, exp), device_id_type=MESH)
    pl.semaphore_wait(barrier, len(peers))


def place():
    me = lax.axis_index("ctx")
    return me, lax.axis_index("exp"), me // (NZ * NC), (me // NC) % NZ, me % NC


def chunk(x, z, core):
    return x * (NZ * NC) + lax.rem(z + 2 * NZ, NZ) * NC + core


def chip(x, z):
    return x * NZ + lax.rem(z + 2 * NZ, NZ)


def hop_copies(w_ref, hop, snd, rcv, slot):
    me, ex, x, z, core = place()
    out = []
    for way, (xx, step) in enumerate(((x, 1), (1 - x, -1))):
        ref = w_ref.at[chip(xx, z - step * hop)]
        out.append(remote(ref, ref, snd.at[slot, way], rcv.at[slot, way], chunk(x, z + step, core), ex))
    return out


def start_hop(*a):
    for c in hop_copies(*a):
        c.start()


def finish_hop(w_ref, hop, snd, rcv, slot):
    me, ex, x, z, core = place()
    for way, (xx, step) in enumerate(((x, 1), (1 - x, -1))):
        ref = w_ref.at[chip(xx, z - step * (hop + 1))]
        remote(ref, ref, snd.at[slot, way], rcv.at[slot, way], me, ex).wait_recv()
    for c in hop_copies(w_ref, hop, snd, rcv, slot):
        c.wait_send()


def ring_peers():
    me, ex, x, z, core = place()
    return [(chunk(x, z + 1, core), ex), (chunk(x, z - 1, core), ex)]


HBM = pltpu.HBM
TILES = FF // NC // 128
FH = FF // NC
CHIPS = CTX // NC
WSHAPE = jax.ShapeDtypeStruct((CHIPS, NC, 3 * FH, 128), BF16)
ATTN_HOPS, PROJ_HOPS = 1, 4
EXPERT_HOPS = NZ - 1 - ATTN_HOPS - PROJ_HOPS


def gather_kernel(
    k_ref, v_ref, q_ref, g_ref, u_ref, d_ref, kv_ref, qm_ref, w_ref,
    local, ring_s, ring_r, sib_s, sib_r, own_s, own_r, w_l, w_s, w_r, wx_s, wx_r,
):
    me, ex, x, z, core = place()

    up, down = chunk(x, z + 1, core), chunk(x, z - 1, core)
    across, sib, mirror = chunk(1 - x, z, core), chunk(x, z, 1 - core), CTX - 1 - me
    head = pl.ds(pl.multiple_of((ex // 2) * HD, HD), HD)
    copies = [
        pltpu.make_async_copy(k_ref.at[:, head], kv_ref.at[me, 0], local.at[0]),
        pltpu.make_async_copy(v_ref.at[:, head], kv_ref.at[me, 1], local.at[1]),
    ]
    here = chip(x, z)

    def pieces(half):
        for a, ref in enumerate((g_ref, u_ref)):
            for t in range(TILES):
                cols = pl.ds(pl.multiple_of(half * FH + t * 128, 128), 128)
                yield ref.at[:, cols], w_ref.at[here, core, pl.ds((a * TILES + t) * 128, 128)]
        yield d_ref.at[pl.ds(pl.multiple_of(half * FH, FH), FH)], w_ref.at[here, core, pl.ds(2 * FH, FH)]

    kept = [pltpu.make_async_copy(src, dst, w_l.at[i]) for i, (src, dst) in enumerate(pieces(core))]
    for c in copies + kept:
        c.start()
    greet([(up, ex), (down, ex), (across, ex), (sib, ex), (mirror, ex)])
    for c in copies:
        c.wait()
    sent = []

    def send(*a):
        c = remote(*a, ex)
        c.start()
        sent.append(c)
        return c

    xs = (x, 1 - x)

    def piece(stream, step):
        which, kv = stream // 2, stream % 2
        zz = z - step if kv == 0 else z + step
        return kv_ref.at[chunk(xs[which], zz, core), kv]

    def hop(stream, step):
        ref = piece(stream, step)
        return send(ref, ref, ring_s.at[stream, step], ring_r.at[stream, step], up if stream % 2 == 0 else down)

    def landed(stream, step):
        ref = piece(stream, step + 1)
        remote(ref, ref, ring_s.at[stream, step], ring_r.at[stream, step], me, ex).wait_recv()

    own = kv_ref.at[me]
    for stream in (0, 1):
        hop(stream, 0)
    a = send(own, own, own_s.at[0], own_r.at[0], across)
    send(own, own, own_s.at[1], own_r.at[1], sib)
    for i, (src, dst) in enumerate(pieces(1 - core)):
        send(src, dst, w_s.at[i], w_r.at[i], sib)
    send(q_ref.at[pl.ds(HALF, HALF)], qm_ref, own_s.at[2], own_r.at[2], mirror)
    other = kv_ref.at[across]
    remote(other, other, own_s.at[0], own_r.at[0], me, ex).wait_recv()
    for stream in (2, 3):
        hop(stream, 0)
    send(other, other, own_s.at[3], own_r.at[3], sib)
    for i, (src, dst) in enumerate(pieces(core)):
        kept[i].wait()
        remote(src, dst, w_s.at[i], w_r.at[i], me, ex).wait_recv()
    send(w_ref.at[here], w_ref.at[here], wx_s, wx_r, across)
    for step in range(NZ - 1):
        for stream in range(4):
            landed(stream, step)
            if step + 1 < NZ - 1:
                hop(stream, step + 1)
            ref = piece(stream, step + 1)
            send(ref, ref, sib_s.at[stream, step], sib_r.at[stream, step], sib)
    for stream in range(4):
        which, kv = stream // 2, stream % 2
        for step in range(NZ - 1):
            zz = z - step - 1 if kv == 0 else z + step + 1
            ref = kv_ref.at[chunk(xs[which], zz, 1 - core), kv]
            remote(ref, ref, sib_s.at[stream, step], sib_r.at[stream, step], me, ex).wait_recv()
    ref = kv_ref.at[sib]
    remote(ref, ref, own_s.at[1], own_r.at[1], me, ex).wait_recv()
    ref = kv_ref.at[chunk(1 - x, z, 1 - core)]
    remote(ref, ref, own_s.at[3], own_r.at[3], me, ex).wait_recv()
    beside = w_ref.at[chip(1 - x, z)]
    remote(beside, beside, wx_s, wx_r, me, ex).wait_recv()
    remote(qm_ref, qm_ref, own_s.at[2], own_r.at[2], me, ex).wait_recv()
    for c in sent:
        c.wait_send()


def gather(keys, values, queries, w_gate, w_up, w_down):
    n = 2 * TILES + 1
    return pl.pallas_call(
        gather_kernel,
        out_shape=(
            jax.ShapeDtypeStruct((CTX, 2, TOK, HD), BF16),
            jax.ShapeDtypeStruct((HALF, HEADS * HD), BF16),
            WSHAPE,
        ),
        in_specs=[pl.BlockSpec(memory_space=pl.ANY)] * 6,
        out_specs=(
            pl.BlockSpec(memory_space=pltpu.VMEM),
            pl.BlockSpec(memory_space=pltpu.VMEM),
            pl.BlockSpec(memory_space=HBM),
        ),
        scratch_shapes=[
            pltpu.SemaphoreType.DMA((2,)),
            pltpu.SemaphoreType.DMA((4, NZ - 1)),
            pltpu.SemaphoreType.DMA((4, NZ - 1)),
            pltpu.SemaphoreType.DMA((4, NZ - 1)),
            pltpu.SemaphoreType.DMA((4, NZ - 1)),
            pltpu.SemaphoreType.DMA((4,)),
            pltpu.SemaphoreType.DMA((4,)),
            pltpu.SemaphoreType.DMA((n,)),
            pltpu.SemaphoreType.DMA((n,)),
            pltpu.SemaphoreType.DMA((n,)),
            pltpu.SemaphoreType.DMA,
            pltpu.SemaphoreType.DMA,
        ],
        compiler_params=pltpu.CompilerParams(collective_id=1, has_side_effects=True, vmem_limit_bytes=16 * MIB),
        cost_estimate=pl.CostEstimate(flops=0, bytes_accessed=64 * MIB, transcendentals=0),
        name="kv_gather",
    )(keys, values, queries, w_gate, w_up, w_down)


KB = 1024
CHUNKS = KB // TOK
TR = 128
QROWS = HEADS * HALF
SCALE2 = math.log2(math.e) / math.sqrt(HD)


def attn_kernel(q_ref, qm_ref, kv_ref, w_in, oa_ref, om_ref, w_ref, qs, acc, m_sc, vx, snd, rcv):
    greet(ring_peers())
    start_hop(w_ref, 0, snd, rcv, 0)
    me = lax.axis_index("ctx")
    starts = (me * TOK, (CTX - 1 - me) * TOK + HALF)
    vx[:, HD:] = jnp.ones((KB, HD), BF16)
    for which, (src, dst) in enumerate(((q_ref, oa_ref), (qm_ref, om_ref))):
        start = starts[which]
        for h in range(HEADS):
            qs[pl.ds(h * HALF, HALF), :] = src[:, pl.ds(h * HD, HD)]
        m_sc[...] = jnp.full_like(m_sc, -1e30)
        acc[...] = jnp.zeros_like(acc)

        def block(j, masked, start=start):
            k = kv_ref[pl.ds(CHUNKS * j, CHUNKS), 0].reshape(KB, HD)
            vx[:, :HD] = kv_ref[pl.ds(CHUNKS * j, CHUNKS), 1].reshape(KB, HD)
            for t in range(QROWS // TR):
                rows = pl.ds(t * TR, TR)
                s = lax.dot_general(qs[rows, :], k, (((1,), (1,)), ((), ())), preferred_element_type=F32)
                if masked:
                    row = lax.broadcasted_iota(jnp.int32, (TR, KB), 0) % HALF + start
                    col = lax.broadcasted_iota(jnp.int32, (TR, KB), 1) + j * KB
                    s = jnp.where(col <= row, s, -1e30)
                old = m_sc[rows, :]
                new = jnp.maximum(old, jnp.max(s, axis=1, keepdims=True))
                p = jnp.exp2((s - new[:, :1]) * SCALE2)
                factor = jnp.exp2((old - new) * SCALE2)
                m_sc[rows, :] = new
                acc[rows, :] = acc[rows, :] * jnp.concatenate([factor, factor], axis=1) + jnp.dot(
                    p.astype(BF16), vx[...], preferred_element_type=F32
                )

        full = start // KB
        lax.fori_loop(0, full, lambda j, c: (block(j, False), c)[1], 0)
        block(full, True)
        for h in range(HEADS):
            rows = pl.ds(h * HALF, HALF)
            dst[:, pl.ds(h * HD, HD)] = (acc[rows, :HD] / acc[rows, HD:]).astype(BF16)
    finish_hop(w_ref, 0, snd, rcv, 0)


def attention(queries, mirrored, kv, weights):
    half = jax.ShapeDtypeStruct((HALF, HEADS * HD), BF16)
    vmem, hbm = pl.BlockSpec(memory_space=pltpu.VMEM), pl.BlockSpec(memory_space=HBM)
    return pl.pallas_call(
        attn_kernel,
        out_shape=(half, half, WSHAPE),
        in_specs=[vmem, vmem, vmem, hbm],
        out_specs=(vmem, vmem, hbm),
        input_output_aliases={3: 2},
        scratch_shapes=[
            pltpu.VMEM((QROWS, HD), BF16),
            pltpu.VMEM((QROWS, 2 * HD), F32),
            pltpu.VMEM((QROWS, HD), F32),
            pltpu.VMEM((KB, 2 * HD), BF16),
            pltpu.SemaphoreType.DMA((ATTN_HOPS, 2)),
            pltpu.SemaphoreType.DMA((ATTN_HOPS, 2)),
        ],
        compiler_params=pltpu.CompilerParams(collective_id=4, has_side_effects=True, vmem_limit_bytes=32 * MIB),
        cost_estimate=pl.CostEstimate(flops=9_000_000_000, bytes_accessed=6 * MIB, transcendentals=9_000_000),
        name="attention",
    )(queries, mirrored, kv, weights)


def slots(ids_ref):
    lane = lax.broadcasted_iota(jnp.int32, (ROWS, EXPERTS * CAP), 1)
    named = [ids_ref[:, k : k + 1] == lane // CAP for k in range(2)]
    has = (named[0] | named[1]).astype(F32)
    tri = lax.broadcasted_iota(jnp.int32, (ROWS, ROWS), 1) < lax.broadcasted_iota(jnp.int32, (ROWS, ROWS), 0)
    place = jnp.dot(tri.astype(F32).astype(BF16), has.astype(BF16), preferred_element_type=F32)
    here = place == (lane % CAP).astype(F32)
    return [(n & here).astype(F32) for n in named]


NB = 512


def project_kernel(
    oa_ref, om_ref, w_hbm, res_ref, gain_ref, ids_ref, e_in, arr_ref, hid_ref, e_ref,
    w, back, part, recv, norm, out, w_sem, back_s, back_r, rs_s, rs_r, a_s, a_r, f_s, f_r, snd, rcv,
):
    me, ex = lax.axis_index("ctx"), lax.axis_index("exp")
    mirror, sib = CTX - 1 - me, me + 1 - 2 * (me % NC)
    load = pltpu.make_async_copy(w_hbm, w, w_sem)
    load.start()
    peers = [lax.rem(ex + d, EXP) for d in range(1, EXP)]
    greet(ring_peers() + [(mirror, ex), (sib, ex)] + [(me, p) for p in peers])
    give = remote(om_ref, back, back_s, back_r, mirror, ex)
    give.start()
    start_hop(e_ref, ATTN_HOPS, snd, rcv, 0)
    load.wait()

    def next_hop(i):
        finish_hop(e_ref, ATTN_HOPS + i, snd, rcv, i)
        if i + 1 < PROJ_HOPS:
            start_hop(e_ref, ATTN_HOPS + i + 1, snd, rcv, i + 1)

    def half(src, first):
        @pl.loop(0, D // NB)
        def _(n):
            cols = pl.ds(pl.multiple_of(n * NB, NB), NB)
            got = jnp.dot(src[...], w[:, cols], preferred_element_type=F32).astype(BF16)
            for b in range(4):
                part[first + b, :, cols] = got[b * ROWS : (b + 1) * ROWS, :]

    def share(d):
        p = lax.rem(ex + d, EXP)
        return p, remote(part.at[p], recv.at[d - 1], rs_s.at[d - 1], rs_r.at[d - 1], me, p)

    def share_half(first):
        for d in range(1, EXP):
            p, copy = share(d)

            @pl.when((p >= first) & (p < first + 4))
            def _():
                copy.start()

    half(oa_ref, 0)
    share_half(0)
    give.wait_recv()
    half(back, 4)
    share_half(4)
    next_hop(0)
    next_hop(1)
    for d in range(1, EXP):
        share(d)[1].wait_recv()

    @pl.loop(0, D // NB)
    def _(n):
        cols = pl.ds(pl.multiple_of(n * NB, NB), NB)
        total = part[ex, :, cols].astype(F32)
        for d in range(EXP - 1):
            total += recv[d, :, cols].astype(F32)
        hid_ref[:, cols] = (res_ref[:, cols].astype(F32) + total).astype(BF16)

    state = hid_ref[...].astype(F32)
    inv = 1.0 / jnp.sqrt(jnp.mean(state * state, axis=1, keepdims=True) + 1e-06)
    norm[...] = (state * inv * gain_ref[...].astype(F32)).astype(BF16)
    first, second = slots(ids_ref)
    table = (first + second).T.astype(BF16)
    out[...] = jnp.dot(table, norm[...], preferred_element_type=F32).astype(BF16).reshape(EXPERTS, CAP, D)

    def give_rows(d):
        p = lax.rem(ex + d, EXP)
        return remote(out.at[p], arr_ref.at[0, ex], a_s.at[d - 1], a_r.at[d - 1], me, p)

    def forward(d):
        source = lax.rem(ex + EXP - d, EXP)
        return remote(arr_ref.at[0, source], arr_ref.at[1, source], f_s.at[d], f_r.at[d], sib, ex)

    for d in range(1, EXP):
        give_rows(d).start()
    arr_ref[0, ex] = out[ex]
    forward(0).start()
    next_hop(2)
    for d in range(1, EXP):
        source = lax.rem(ex + EXP - d, EXP)
        remote(out.at[ex], arr_ref.at[0, source], a_s.at[d - 1], a_r.at[d - 1], me, ex).wait_recv()
        forward(d).start()
    for d in range(EXP):
        forward(d).wait()
    next_hop(3)
    give.wait_send()
    for d in range(1, EXP):
        share(d)[1].wait_send()
        give_rows(d).wait_send()


def project(attn_own, attn_mirror, w_out, residual, gain, ids, weights):
    vmem, any_ = pl.BlockSpec(memory_space=pltpu.VMEM), pl.BlockSpec(memory_space=pl.ANY)
    return pl.pallas_call(
        project_kernel,
        out_shape=(
            jax.ShapeDtypeStruct((NC, EXPERTS, CAP, D), BF16),
            jax.ShapeDtypeStruct((ROWS, D), BF16),
            WSHAPE,
        ),
        in_specs=[vmem, vmem, any_, vmem, vmem, vmem, pl.BlockSpec(memory_space=HBM)],
        out_specs=(vmem, vmem, pl.BlockSpec(memory_space=HBM)),
        input_output_aliases={6: 2},
        scratch_shapes=[
            pltpu.VMEM((HEADS * HD, D), BF16),
            pltpu.VMEM((HALF, HEADS * HD), BF16),
            pltpu.VMEM((EXP, ROWS, D), BF16),
            pltpu.VMEM((EXP - 1, ROWS, D), BF16),
            pltpu.VMEM((ROWS, D), BF16),
            pltpu.VMEM((EXPERTS, CAP, D), BF16),
            pltpu.SemaphoreType.DMA,
            pltpu.SemaphoreType.DMA,
            pltpu.SemaphoreType.DMA,
            pltpu.SemaphoreType.DMA((EXP - 1,)),
            pltpu.SemaphoreType.DMA((EXP - 1,)),
            pltpu.SemaphoreType.DMA((EXP - 1,)),
            pltpu.SemaphoreType.DMA((EXP - 1,)),
            pltpu.SemaphoreType.DMA((EXP,)),
            pltpu.SemaphoreType.DMA((EXP,)),
            pltpu.SemaphoreType.DMA((PROJ_HOPS, 2)),
            pltpu.SemaphoreType.DMA((PROJ_HOPS, 2)),
        ],
        compiler_params=pltpu.CompilerParams(collective_id=2, has_side_effects=True, vmem_limit_bytes=40 * MIB),
        cost_estimate=pl.CostEstimate(flops=2_200_000_000, bytes_accessed=64 * MIB, transcendentals=0),
        name="project_dispatch",
    )(attn_own, attn_mirror, w_out, residual, gain, ids, weights)


SLOTS = EXPERTS * CAP
DEPTH = NC * 128
GROUPS = 4
GCOLS = D // GROUPS


def expert_kernel(
    arr_ref, w_in, hid_ref, ids_ref, gates_ref, o_ref, w_hbm,
    w, pre, act, mine, theirs, other, res, got, w_sem, x_s, x_r, r_s, r_r, snd, rcv,
):
    me, ex, x, z, core = place()
    sib = me + 1 - 2 * core
    held = ATTN_HOPS + PROJ_HOPS + 1

    def load(step, way):
        c = chip(x, z - step) if way == 0 else chip(1 - x, z + step)
        return c, pltpu.make_async_copy(w_hbm.at[c], w.at[c], w_sem.at[step, way])

    for step in range(held):
        for way in range(2):
            load(step, way)[1].start()
    peers = [lax.rem(ex + d, EXP) for d in range(1, EXP)]
    greet(ring_peers() + [(sib, ex)] + [(me, p) for p in peers])
    start_hop(w_hbm, held - 1, snd, rcv, 0)
    pre[...] = jnp.zeros_like(pre)

    def use(step):
        for way in range(2):
            j, copy = load(step, way)
            copy.wait()
            cols = pl.ds(pl.multiple_of(j * DEPTH, DEPTH), DEPTH)
            rows = arr_ref[:, :, :, cols].reshape(NC * SLOTS, DEPTH)
            tiles = [
                jnp.concatenate([w[j, c, pl.ds(t * 128, 128)] for c in range(NC)], axis=0) for t in range(2 * TILES)
            ]
            pre[...] += jnp.dot(rows, jnp.concatenate(tiles, axis=1), preferred_element_type=F32)

    @pl.loop(0, held)
    def _(step):
        use(step)

    for i in range(EXPERT_HOPS):
        finish_hop(w_hbm, held - 1 + i, snd, rcv, i)
        if i + 1 < EXPERT_HOPS:
            start_hop(w_hbm, held + i, snd, rcv, i + 1)
        for way in range(2):
            load(held + i, way)[1].start()
        use(held + i)

    gate = pre[:, :FH]
    act[...] = (gate / (1.0 + jnp.exp(-gate)) * pre[:, FH:]).astype(BF16)
    per = CHIPS // GROUPS

    def swap(g):
        return remote(theirs.at[g], other.at[g], x_s.at[g], x_r.at[g], sib, ex)

    def give(g, d):
        p = lax.rem(ex + d, EXP)
        return remote(res.at[g, p], got.at[g, ex], r_s.at[g, d - 1], r_r.at[g, d - 1], me, p)

    def finish(g):
        swap(g).wait_recv()
        res[g] = (mine[g] + other[g]).astype(BF16).reshape(EXPERTS, CAP, GCOLS)
        for d in range(1, EXP):
            give(g, d).start()
        got[g, ex] = res[g, ex]

    for g in range(GROUPS):

        @pl.loop(0, per)
        def _(j):
            down = jnp.concatenate([w[g * per + j, c, pl.ds(2 * FH, FH)] for c in range(NC)], axis=1)
            made = jnp.dot(act[...], down, preferred_element_type=F32)
            cols = pl.ds(pl.multiple_of(j * DEPTH, DEPTH), DEPTH)
            mine[g, :, cols] = made[:SLOTS]
            theirs[g, :, cols] = made[SLOTS:]

        swap(g).start()
        if g >= 1:
            finish(g - 1)
    finish(GROUPS - 1)

    first, second = slots(ids_ref)
    picks = jnp.concatenate([first, second], axis=0).astype(BF16)
    weight = [gates_ref[:, k : k + 1] for k in range(2)]
    for g in range(GROUPS):
        for d in range(1, EXP):
            source = lax.rem(ex + EXP - d, EXP)
            remote(res.at[g, ex], got.at[g, source], r_s.at[g, d - 1], r_r.at[g, d - 1], me, ex).wait_recv()
        both = jnp.dot(picks, got[g].reshape(SLOTS, GCOLS), preferred_element_type=F32)
        total = weight[0] * both[:ROWS] + weight[1] * both[ROWS:]
        cols = pl.ds(g * GCOLS, GCOLS)
        o_ref[:, cols] = (hid_ref[:, cols].astype(F32) + total).astype(BF16)
    for g in range(GROUPS):
        swap(g).wait_send()
        for d in range(1, EXP):
            give(g, d).wait_send()


def experts(arrived, weights, hidden, ids, gates):
    vmem, hbm = pl.BlockSpec(memory_space=pltpu.VMEM), pl.BlockSpec(memory_space=HBM)
    return pl.pallas_call(
        expert_kernel,
        out_shape=(jax.ShapeDtypeStruct((ROWS, D), BF16), WSHAPE),
        in_specs=[vmem, hbm, vmem, vmem, vmem],
        out_specs=(vmem, hbm),
        input_output_aliases={1: 1},
        scratch_shapes=[
            pltpu.VMEM((CHIPS, NC, 3 * FH, 128), BF16),
            pltpu.VMEM((NC * SLOTS, 2 * FH), F32),
            pltpu.VMEM((NC * SLOTS, FH), BF16),
            pltpu.VMEM((GROUPS, SLOTS, GCOLS), F32),
            pltpu.VMEM((GROUPS, SLOTS, GCOLS), F32),
            pltpu.VMEM((GROUPS, SLOTS, GCOLS), F32),
            pltpu.VMEM((GROUPS, EXPERTS, CAP, GCOLS), BF16),
            pltpu.VMEM((GROUPS, EXPERTS, CAP, GCOLS), BF16),
            pltpu.SemaphoreType.DMA((NZ, 2)),
            pltpu.SemaphoreType.DMA((GROUPS,)),
            pltpu.SemaphoreType.DMA((GROUPS,)),
            pltpu.SemaphoreType.DMA((GROUPS, EXP - 1)),
            pltpu.SemaphoreType.DMA((GROUPS, EXP - 1)),
            pltpu.SemaphoreType.DMA((EXPERT_HOPS, 2)),
            pltpu.SemaphoreType.DMA((EXPERT_HOPS, 2)),
        ],
        compiler_params=pltpu.CompilerParams(collective_id=3, has_side_effects=True, vmem_limit_bytes=48 * MIB),
        cost_estimate=pl.CostEstimate(flops=2_500_000_000, bytes_accessed=32 * MIB, transcendentals=100_000),
        name="experts",
    )(arrived, weights, hidden, ids, gates)[0]


def body(queries, keys, values, w_out, residual, norm_gain, expert_ids, gate_weights, w_gate, w_up, w_down):
    kv, mirrored, weights = gather(keys, values, queries, w_gate[0], w_up[0], w_down[0])
    attn_own, attn_mirror, weights = attention(queries[:HALF], mirrored, kv, weights)
    arrived, hidden, weights = project(
        attn_own, attn_mirror, w_out, residual, norm_gain.reshape(1, D), expert_ids, weights
    )
    return experts(arrived, weights, hidden, expert_ids, gate_weights)


def solution(mesh):
    placed = (
        P("ctx", "exp"),
        P("ctx", None),
        P("ctx", None),
        P("exp", None),
        P(("ctx", "exp"), None),
        P(),
        P(("ctx", "exp"), None),
        P(("ctx", "exp"), None),
        P("exp", "ctx", None),
        P("exp", "ctx", None),
        P("exp", None, "ctx"),
    )
    return jax.shard_map(
        body, mesh=mesh, in_specs=placed, out_specs=P(("ctx", "exp"), None), check_vma=False
    )
```

time: 574 us -> 206 us (0.36)
  waiting for transfers between devices: 468 us -> 0 us
  Pallas kernels: 0 us -> 192 us
  blocking collectives: 40.6 us -> 0 us
  matrix products: 22.3 us -> 0 us
  between operations: 13.7 us -> 0.11 us
  local copies, waits for them, and re-layouts: 21.8 us -> 13.7 us
    all_gather x5 -> x0, waiting for transfers between devices: 334 us -> none  [the longest x1 82 us: body(): lax.all_gather(down_local, 'ctx', axis=1, tiled=True)]
    pallas_call x0 -> x4, Pallas kernels: none -> 192 us  [the longest x1 75.8 us: project(): pl.pallas_call(project_kernel, out_shape=(jax.ShapeDtypeStruct((NC, EXPER...]
    reduce_scatter x1 -> x0, waiting for transfers between devices: 132 us -> none  [body(): lax.psum_scatter(jnp.dot(attn, w_out, preferred_element_type=jnp.float32)...]
    all_to_all x2 -> x0, blocking collectives: 40.6 us -> none  [the longest x1 22.1 us: body(): lax.all_to_all(expert_result.reshape(experts_all, capacity, D), 'exp', sp...]
    dot_general x9 -> x0, matrix products: 22.3 us -> none  [the longest x1 7.06 us: body(): jnp.dot(attn, w_out, preferred_element_type=jnp.float32)]
    dynamic_slice x18 -> x0, local copies, waits for them, and re-layouts: 18 us -> none  [the longest x16 15.9 us: one_block(): value_block = lax.dynamic_slice_in_dim(value_piece, key_start, width, 0)]
    unnamed x17 -> x27, local copies, waits for them, and re-layouts: 1.76 us -> 13.6 us
  transfers between devices with their start and end apart: 6 -> 0, of which waited for: 6 -> 0; matrix products, arithmetic and copies ran while one was open for 2% -> 0% of each run, Pallas kernels for 0% -> 0%
where the time goes in v1:
time: 206 us
  Pallas kernels  192 us (93%)
  local copies, waits for them, and re-layouts  13.7 us (7%)
    pallas_call x1, Pallas kernels, project(): pl.pallas_call(project_kernel, out_shape=(jax.ShapeDtypeStruct((NC, EXPER...  75.8 us
    pallas_call x1, Pallas kernels, experts(): pl.pallas_call(expert_kernel, out_shape=(jax.ShapeDtypeStruct((ROWS, D),...  49.3 us
    pallas_call x1, Pallas kernels, gather(): pl.pallas_call(gather_kernel, out_shape=(jax.ShapeDtypeStruct((CTX, 2, TO...  48.9 us
    pallas_call x1, Pallas kernels, attention(): pl.pallas_call(attn_kernel, out_shape=(half, half, WSHAPE), in_specs=[vme...  18.2 us
    unnamed x27, local copies, waits for them, and re-layouts  13.6 us

profile of v1, /device:TPU:1, one launch (start us, length us, event | category | flops | bytes accessed | tf_op | source)
XLA Modules:
  0.0 205.9 jit_solution(11712819704593121491)
XLA Ops:
  0.0 0.0 copy-start.2
  0.0 1.0 copy-done.2
  1.0 0.0 copy-start.4
  1.0 0.9 copy-done.4
  2.0 0.0 copy-start.5
  2.0 0.9 copy-done.5
  2.9 0.0 copy-start.6
  2.9 0.9 copy-done.6
  3.9 0.0 copy-start.7
  3.9 0.9 copy-done.7
  4.8 0.0 copy-start.8
  4.8 0.9 copy-done.8
  5.7 48.9 %kv_gather.1 = (bf16[32,2,256,128]{3,2,1,0:T(8,128)(2,1)S(1)}, bf16[128,1024]{1,0:T(8,128)(2,1)S(1)}, bf16[16,2,1152,128]{3,2,1,0:T(8,128)(2,1)S(1)}) custom-call(bf16[256,512]{1,0:T(8,128)(2,1)S(1)} %copy-done.4, bf16[256,512]{1,0:T(8,128)(2,1)S(1)} %copy-done.5, bf16[256,1024]{1,0:T(8,128)(2,1)S(1)} %copy-done.2, bf16[128,768]{1,0:T(8,128)(2,1)S(1)} %bitcast.3, ...), custom_call_target="tpu_custom_call" | custom-call | bytes 67108864 | tf_op jit(solution)/shard_map/kv_gather/pallas_call | solution.py:188
  54.7 0.0 copy-start.10
  54.7 0.0 copy-start.9
  54.7 0.0 copy-start.3
  54.7 18.2 %attention.1 = (bf16[128,1024]{1,0:T(8,128)(2,1)S(1)}, bf16[128,1024]{1,0:T(8,128)(2,1)S(1)}, bf16[16,2,1152,128]{3,2,1,0:T(8,128)(2,1)S(1)}) custom-call(bf16[128,1024]{1,0:T(8,128)(2,1)S(1)} %slice.3.q_ref, bf16[128,1024]{1,0:T(8,128)(2,1)S(1)} %get-tuple-element.15.qm_ref, ...), custom_call_target="tpu_custom_call", output_to_operand_aliasing={{2}: (3, {})} | custom-call | flops 8999999488 | bytes 6291456 | tf_op jit(solution)/shard_map/attention/pallas_call | solution.py:272
  73.0 0.0 copy-start
  73.0 3.6 %copy-done = bf16[16,2,1152,128]{3,2,1,0:T(8,128)(2,1)} copy-done((bf16[16,2,1152,128]{3,2,1,0:T(8,128)(2,1)}, bf16[16,2,1152,128]{3,2,1,0:T(8,128)(2,1)S(1)}, u32[]{:S(2)}) %copy-start) | copy-done | bytes 9437208
  76.6 0.0 copy-start.11
  76.6 0.0 copy-done.10
  76.6 0.1 copy.15.ids_ref
  76.7 0.0 copy-done.9
  76.7 0.0 copy-done.3
  76.7 0.0 copy-start.1
  76.7 3.4 %copy-done.1 = bf16[1024,4096]{1,0:T(8,128)(2,1)S(1)} copy-done((bf16[1024,4096]{1,0:T(8,128)(2,1)S(1)}, bf16[1024,4096]{1,0:T(8,128)(2,1)}, u32[]{:S(2)}) %copy-start.1) | copy-done | bytes 8388632
  80.1 75.8 %project_dispatch.1 = (bf16[2,8,16,4096]{3,2,1,0:T(8,128)(2,1)S(1)}, bf16[32,4096]{1,0:T(8,128)(2,1)S(1)}, bf16[16,2,1152,128]{3,2,1,0:T(8,128)(2,1)}) custom-call(bf16[128,1024]{1,0:T(8,128)(2,1)S(1)} %get-tuple-element.18.oa_ref, bf16[128,1024]{1,0:T(8,128)(2,1)S(1)} %get-tuple-element.19.om_ref, ...), custom_call_target="tpu_custom_call", output_to_operand_aliasing={{2}: (6, {})} | custom-call | flops 2200000000 | bytes 67108864 | tf_op jit(solution)/shard_map/project_dispatch/pallas_call | solution.py:398
  155.9 0.0 copy-done.11
  155.9 0.1 copy.17.gates_ref
  156.0 49.3 %experts.1 = (bf16[32,4096]{1,0:T(8,128)(2,1)S(1)}, bf16[16,2,1152,128]{3,2,1,0:T(8,128)(2,1)}) custom-call(bf16[2,8,16,4096]{3,2,1,0:T(8,128)(2,1)S(1)} %get-tuple-element.21.arr_ref, bf16[16,2,1152,128]{3,2,1,0:T(8,128)(2,1)} %get-tuple-element.22.w_in, bf16[32,4096]{1,0:T(8,128)(2,1)S(1)} %get-tuple-element.23.hid_ref, ...), custom_call_target="tpu_custom_call", output_to_operand_aliasing={{1}: (1, {})} | custom-call | flops 2500000000 | bytes 33554432 | tf_op jit(solution)/shard_map/experts/pallas_call | solution.py:534
  205.2 0.7 copy.22
  (2 shorter events, 0.0 us)
Async XLA Ops:
  0.0 1.0 copy-start.2
  1.0 0.9 copy-start.4
  2.0 0.9 copy-start.5
  2.9 0.9 copy-start.6
  3.9 0.9 copy-start.7
  4.8 0.9 copy-start.8
  54.7 21.9 %copy-start.10 = (s32[32,2]{0,1:T(2,128)S(1)}, s32[32,2]{0,1:T(2,128)}, u32[]{:S(2)}) copy-start(s32[32,2]{0,1:T(2,128)} %param.17) | copy-start | bytes 772
  54.7 22.0 %copy-start.9 = (bf16[4096]{0:T(1024)(128)(2,1)S(1)}, bf16[4096]{0:T(1024)(128)(2,1)}, u32[]{:S(2)}) copy-start(bf16[4096]{0:T(1024)(128)(2,1)} %param.16) | copy-start | bytes 24580
  54.7 22.0 %copy-start.3 = (bf16[32,4096]{1,0:T(8,128)(2,1)S(1)}, bf16[32,4096]{1,0:T(8,128)(2,1)}, u32[]{:S(2)}) copy-start(bf16[32,4096]{1,0:T(8,128)(2,1)} %res_ref.1) | copy-start | bytes 786436
  73.0 3.7 %copy-start = (bf16[16,2,1152,128]{3,2,1,0:T(8,128)(2,1)}, bf16[16,2,1152,128]{3,2,1,0:T(8,128)(2,1)S(1)}, u32[]{:S(2)}) copy-start(bf16[16,2,1152,128]{3,2,1,0:T(8,128)(2,1)S(1)} %get-tuple-element.20.e_in) | copy-start | bytes 28311556
  76.6 79.3 %copy-start.11 = (f32[32,2]{0,1:T(2,128)S(1)}, f32[32,2]{0,1:T(2,128)}, u32[]{:S(2)}) copy-start(f32[32,2]{0,1:T(2,128)} %param.18) | copy-start | bytes 772
  76.7 3.4 %copy-start.1 = (bf16[1024,4096]{1,0:T(8,128)(2,1)S(1)}, bf16[1024,4096]{1,0:T(8,128)(2,1)}, u32[]{:S(2)}) copy-start(bf16[1024,4096]{1,0:T(8,128)(2,1)} %w_hbm.1) | copy-start | bytes 25165828

commit v2 on v1

v2 whole, which is shorter than its diff:
```python
import functools
import math

import jax
import jax.numpy as jnp
from jax import lax
from jax.experimental import pallas as pl
from jax.experimental.pallas import tpu as pltpu
from jax.sharding import PartitionSpec as P

D = 4096
HQ = 64
KVH = 4
HD = 128
FF = 768
EXPERTS = 8
CAP = 16
ROWS = 32
NX, NZ, NC = 2, 8, 2
CTX = NX * NZ * NC
EXP = 8
TOK = 256
HALF = 128
HEADS = HQ // EXP
MESH = pl.DeviceIdType.MESH
MIB = 1 << 20
F32 = jnp.float32
BF16 = jnp.bfloat16


def remote(src, dst, send, recv, ctx, exp):
    return pltpu.make_async_remote_copy(
        src_ref=src, dst_ref=dst, send_sem=send, recv_sem=recv, device_id=(ctx, exp), device_id_type=MESH
    )


def greet(peers):
    barrier = pltpu.get_barrier_semaphore()
    for ctx, exp in peers:
        pl.semaphore_signal(barrier, inc=1, device_id=(ctx, exp), device_id_type=MESH)
    pl.semaphore_wait(barrier, len(peers))


def place():
    me = lax.axis_index("ctx")
    return me, lax.axis_index("exp"), me // (NZ * NC), (me // NC) % NZ, me % NC


def chunk(x, z, core):
    return x * (NZ * NC) + lax.rem(z + 2 * NZ, NZ) * NC + core


def chip(x, z):
    return x * NZ + lax.rem(z + 2 * NZ, NZ)


def hop_copies(w_ref, kind, hop, snd, rcv, slot):
    me, ex, x, z, core = place()
    out = []
    for way, (xx, step) in enumerate(((x, 1), (1 - x, -1))):
        ref = w_ref.at[chip(xx, z - step * hop), :, kind]
        out.append(remote(ref, ref, snd.at[slot, way], rcv.at[slot, way], chunk(x, z + step, core), ex))
    return out


def start_hop(*a):
    for c in hop_copies(*a):
        c.start()


def finish_hop(w_ref, kind, hop, snd, rcv, slot):
    me, ex, x, z, core = place()
    for way, (xx, step) in enumerate(((x, 1), (1 - x, -1))):
        ref = w_ref.at[chip(xx, z - step * (hop + 1)), :, kind]
        remote(ref, ref, snd.at[slot, way], rcv.at[slot, way], me, ex).wait_recv()
    for c in hop_copies(w_ref, kind, hop, snd, rcv, slot):
        c.wait_send()


def ring_peers():
    me, ex, x, z, core = place()
    return [(chunk(x, z + 1, core), ex), (chunk(x, z - 1, core), ex)]


HBM = pltpu.HBM
TILES = FF // NC // 128
FH = FF // NC
CHIPS = CTX // NC
WSHAPE = HBM((CHIPS, NC, 3 * FH, 128), BF16)


def in_hbm(x):
    return pltpu.with_memory_space_constraint(x, HBM)


PRE, DOWN = pl.ds(0, 2 * FH), pl.ds(2 * FH, FH)
ATTN_HOPS, PROJ_HOPS = 1, 5
ATTN_DOWN, PROJ_DOWN = 1, 2
EXPERT_HOPS = NZ - 1 - ATTN_HOPS - PROJ_HOPS
DOWN_HELD = ATTN_DOWN + PROJ_DOWN + 1


CK = NC * TOK
KB = 2 * CK
TR = 128
QROWS = HEADS * HALF
SCALE2 = math.log2(math.e) / math.sqrt(HD)
NP = 2 * TILES + 1


def attn_kernel(
    q_ref, k_ref, v_ref, g_ref, u_ref, d_ref, o_ref, w_ref,
    kv, qs, acc, m_sc, vx,
    kv_l, q_l, own_s, own_r, ring_s, ring_r, sib_s, sib_r, w_l, w_s, w_r, wx_s, wx_r, snd, rcv, d_s, d_r,
):
    me, ex, x, z, core = place()
    up, down = chunk(x, z + 1, core), chunk(x, z - 1, core)
    across, sib = chunk(1 - x, z, core), chunk(x, z, 1 - core)
    here = chip(x, z)
    head = pl.ds(pl.multiple_of((ex // 2) * HD, HD), HD)

    def part(c, cc):
        return kv.at[c, :, pl.ds(pl.multiple_of(cc * TOK, TOK), TOK)]

    def pieces(half):
        for a, ref in enumerate((g_ref, u_ref)):
            for t in range(TILES):
                cols = pl.ds(pl.multiple_of(half * FH + t * 128, 128), 128)
                yield ref.at[:, cols], w_ref.at[here, core, pl.ds((a * TILES + t) * 128, 128)]
        yield d_ref.at[pl.ds(pl.multiple_of(half * FH, FH), FH)], w_ref.at[here, core, pl.ds(2 * FH, FH)]

    rows0 = pl.ds(pl.multiple_of(core * TOK, TOK), TOK)
    kvl = [
        pltpu.make_async_copy(ref.at[:, head], kv.at[here, i, rows0], kv_l.at[i]) for i, ref in enumerate((k_ref, v_ref))
    ]
    ql = [
        pltpu.make_async_copy(
            q_ref.at[pl.ds(a * HALF, HALF), pl.ds(h * HD, HD)], qs.at[a, pl.ds(h * HALF, HALF)], q_l.at[a, h]
        )
        for a in range(2)
        for h in range(HEADS)
    ]
    kept = [pltpu.make_async_copy(src, dst, w_l.at[i]) for i, (src, dst) in enumerate(pieces(core))]
    for c in kvl + ql + kept:
        c.start()
    greet([(up, ex), (down, ex), (across, ex), (sib, ex)])
    for c in kvl:
        c.wait()

    def piece(way, step, cc):
        return part(chip(x, z - step) if way == 0 else chip(1 - x, z + step), cc)

    def hop(way, step):
        ref = piece(way, step, core)
        return remote(ref, ref, ring_s.at[way, step], ring_r.at[way, step], up if way == 0 else down, ex)

    def share(way, step):
        ref = piece(way, step, core)
        return remote(ref, ref, sib_s.at[way, step], sib_r.at[way, step], sib, ex)

    def shared(way, step):
        ref = piece(way, step, 1 - core)
        remote(ref, ref, sib_s.at[way, step], sib_r.at[way, step], me, ex).wait_recv()

    own = part(here, core)
    cross = remote(own, own, own_s, own_r, across, ex)
    cross.start()
    hop(0, 0).start()
    share(0, 0).start()
    other = part(chip(1 - x, z), core)
    remote(other, other, own_s, own_r, me, ex).wait_recv()
    hop(1, 0).start()
    share(1, 0).start()
    wsent = [remote(src, dst, w_s.at[i], w_r.at[i], sib, ex) for i, (src, dst) in enumerate(pieces(1 - core))]
    for c in wsent:
        c.start()
    wcross = remote(w_ref.at[here], w_ref.at[here], wx_s, wx_r, across, ex)
    vx[:, HD:] = jnp.ones((KB, HD), BF16)
    m_sc[...] = jnp.full_like(m_sc, -1e30)
    acc[...] = jnp.zeros_like(acc)
    for c in ql:
        c.wait()

    def block(which, start, c0, c1, masked):
        k = jnp.concatenate([kv[c0, 0], kv[c1, 0]], axis=0)
        for t in range(QROWS // TR):
            rows = pl.ds(t * TR, TR)
            s = lax.dot_general(qs[which, rows, :], k, (((1,), (1,)), ((), ())), preferred_element_type=F32)
            if masked:
                row = lax.broadcasted_iota(jnp.int32, (TR, KB), 0) % HALF + start
                lane = lax.broadcasted_iota(jnp.int32, (TR, KB), 1)
                col = lane + jnp.where(lane < CK, c0 * CK, c1 * CK - CK)
                s = jnp.where(col <= row, s, -1e30)
            old = m_sc[which, rows, :]
            new = jnp.maximum(old, jnp.max(s, axis=1, keepdims=True))
            p = jnp.exp2((s - new[:, :1]) * SCALE2)
            factor = jnp.exp2((old - new) * SCALE2)
            m_sc[which, rows, :] = new
            acc[which, rows, :] = acc[which, rows, :] * jnp.concatenate([factor, factor], axis=1) + jnp.dot(
                p.astype(BF16), vx[...], preferred_element_type=F32
            )

    @pl.loop(0, NZ + 1)
    def _(u):
        step = u + 1

        @pl.when(step < NZ)
        def _():
            for way in range(2):
                ref = piece(way, step, core)
                remote(ref, ref, ring_s.at[way, step - 1], ring_r.at[way, step - 1], me, ex).wait_recv()

                @pl.when(step < NZ - 1)
                def _():
                    hop(way, step).start()

                share(way, step).start()

        @pl.when(u == 2)
        def _():
            for i in range(NP):
                kept[i].wait()
                wsent[i].wait_recv()
            wcross.start()

        @pl.when(u == NZ - 2)
        def _():
            wcross.wait_recv()
            start_hop(w_ref, PRE, 0, snd, rcv, 0)
            start_hop(w_ref, DOWN, 0, d_s, d_r, 0)

        turn = u - 1
        way = lax.rem(turn + 2, 2)
        pair = turn - way

        @pl.when(turn >= 0)
        def _():
            mine = way == 0
            for w in range(2):

                @pl.when(way == w)
                def _():
                    shared(w, pair)
                    shared(w, pair + 1)

            c0 = jnp.where(mine, chip(x, z - pair), chip(1 - x, z + pair))
            c1 = jnp.where(mine, chip(x, z - pair - 1), chip(1 - x, z + pair + 1))
            vx[pl.ds(0, CK), :HD] = kv[c0, 1]
            vx[pl.ds(CK, CK), :HD] = kv[c1, 1]

            @pl.loop(0, 2)
            def _(which):
                start = me * TOK + which * HALF
                full = jnp.maximum(c0, c1) * CK + CK - 1 <= start
                some = jnp.minimum(c0, c1) * CK <= start

                @pl.when(full)
                def _():
                    block(which, start, c0, c1, False)

                @pl.when(some & jnp.logical_not(full))
                def _():
                    block(which, start, c0, c1, True)

    for which in range(2):
        for h in range(HEADS):
            rows = pl.ds(h * HALF, HALF)
            made = (acc[which, rows, :HD] / acc[which, rows, HD:]).astype(BF16)
            o_ref[pl.ds(which * HALF, HALF), pl.ds(h * HD, HD)] = made
    finish_hop(w_ref, PRE, 0, snd, rcv, 0)
    finish_hop(w_ref, DOWN, 0, d_s, d_r, 0)
    cross.wait_send()
    wcross.wait_send()
    for c in wsent:
        c.wait_send()
    for way in range(2):
        for step in range(NZ):
            share(way, step).wait_send()
            if step < NZ - 1:
                hop(way, step).wait_send()


def attention(queries, keys, values, w_gate, w_up, w_down):
    dma = pltpu.SemaphoreType.DMA
    hbm = pl.BlockSpec(memory_space=HBM)
    return pl.pallas_call(
        attn_kernel,
        out_shape=(jax.ShapeDtypeStruct((TOK, HEADS * HD), BF16), WSHAPE),
        in_specs=[hbm] * 6,
        out_specs=(pl.BlockSpec(memory_space=pltpu.VMEM), hbm),
        scratch_shapes=[
            pltpu.VMEM((CHIPS, 2, CK, HD), BF16),
            pltpu.VMEM((2, QROWS, HD), BF16),
            pltpu.VMEM((2, QROWS, 2 * HD), F32),
            pltpu.VMEM((2, QROWS, HD), F32),
            pltpu.VMEM((KB, 2 * HD), BF16),
            dma((2,)), dma((2, HEADS)),
            dma, dma,
            dma((2, NZ - 1)), dma((2, NZ - 1)), dma((2, NZ)), dma((2, NZ)),
            dma((NP,)), dma((NP,)), dma((NP,)), dma, dma,
            dma((ATTN_HOPS, 2)), dma((ATTN_HOPS, 2)), dma((ATTN_DOWN, 2)), dma((ATTN_DOWN, 2)),
        ],
        compiler_params=pltpu.CompilerParams(collective_id=1, has_side_effects=True, vmem_limit_bytes=32 * MIB),
        cost_estimate=pl.CostEstimate(flops=9_000_000_000, bytes_accessed=64 * MIB, transcendentals=9_000_000),
        name="attention",
    )(*(in_hbm(a) for a in (queries, keys, values, w_gate, w_up, w_down)))


def slots(ids_ref):
    lane = lax.broadcasted_iota(jnp.int32, (ROWS, EXPERTS * CAP), 1)
    named = [ids_ref[:, k : k + 1] == lane // CAP for k in range(2)]
    has = (named[0] | named[1]).astype(F32)
    tri = lax.broadcasted_iota(jnp.int32, (ROWS, ROWS), 1) < lax.broadcasted_iota(jnp.int32, (ROWS, ROWS), 0)
    place = jnp.dot(tri.astype(F32).astype(BF16), has.astype(BF16), preferred_element_type=F32)
    here = place == (lane % CAP).astype(F32)
    return [(n & here).astype(F32) for n in named]


NB = 512
PG = 2
PC = D // PG
WL = D // NB


def project_kernel(
    o_ref, w_hbm, res_ref, gain_ref, ids_ref, e_in, arr_ref, hid_ref, e_ref,
    w, part, recv, norm, out, w_sem, rs_s, rs_r, a_s, a_r, f_s, f_r, snd, rcv, d_s, d_r,
):
    me, ex, x, z, core = place()
    sib = me + 1 - 2 * core

    def load(n):
        cols = pl.ds(pl.multiple_of(n * NB, NB), NB)
        return pltpu.make_async_copy(w_hbm.at[:, cols], w.at[n], w_sem.at[n])

    for n in range(WL):
        load(n).start()
    peers = [lax.rem(ex + d, EXP) for d in range(1, EXP)]
    greet(ring_peers() + [(sib, ex)] + [(me, p) for p in peers])
    start_hop(e_ref, PRE, ATTN_HOPS, snd, rcv, 0)
    start_hop(e_ref, DOWN, ATTN_DOWN, d_s, d_r, 0)

    def next_down(i):
        finish_hop(e_ref, DOWN, ATTN_DOWN + i, d_s, d_r, i)
        if i + 1 < PROJ_DOWN:
            start_hop(e_ref, DOWN, ATTN_DOWN + i + 1, d_s, d_r, i + 1)

    def next_hop(i):
        finish_hop(e_ref, PRE, ATTN_HOPS + i, snd, rcv, i)
        if i + 1 < PROJ_HOPS:
            start_hop(e_ref, PRE, ATTN_HOPS + i + 1, snd, rcv, i + 1)

    def share(g, d):
        p = lax.rem(ex + d, EXP)
        return remote(part.at[g, p], recv.at[g, d - 1], rs_s.at[g, d - 1], rs_r.at[g, d - 1], me, p)

    for g in range(PG):

        @pl.loop(0, PC // NB)
        def _(i):
            n = g * (PC // NB) + i
            load(n).wait()
            got = jnp.dot(o_ref[...], w[n], preferred_element_type=F32).astype(BF16)
            cols = pl.ds(pl.multiple_of(i * NB, NB), NB)
            for b in range(EXP):
                part[g, b, :, cols] = got[b * ROWS : (b + 1) * ROWS, :]

        for d in range(1, EXP):
            share(g, d).start()

    next_hop(0)
    for g in range(PG):
        if g == 0:
            next_hop(1)
            next_down(0)
        for d in range(1, EXP):
            share(g, d).wait_recv()

        @pl.loop(0, PC // NB)
        def _(i):
            cols = pl.ds(pl.multiple_of(i * NB, NB), NB)
            total = part[g, ex, :, cols].astype(F32)
            for d in range(EXP - 1):
                total += recv[g, d, :, cols].astype(F32)
            full = pl.ds(pl.multiple_of(g * PC + i * NB, NB), NB)
            hid_ref[:, full] = (res_ref[:, full].astype(F32) + total).astype(BF16)

    state = hid_ref[...].astype(F32)
    inv = 1.0 / jnp.sqrt(jnp.mean(state * state, axis=1, keepdims=True) + 1e-06)
    norm[...] = (state * inv * gain_ref[...].astype(F32)).astype(BF16)
    first, second = slots(ids_ref)
    table = (first + second).T.astype(BF16)
    out[...] = jnp.dot(table, norm[...], preferred_element_type=F32).astype(BF16).reshape(EXPERTS, CAP, D)

    def give_rows(d):
        p = lax.rem(ex + d, EXP)
        return remote(out.at[p], arr_ref.at[0, ex], a_s.at[d - 1], a_r.at[d - 1], me, p)

    def forward(d):
        source = lax.rem(ex + EXP - d, EXP)
        return remote(arr_ref.at[0, source], arr_ref.at[1, source], f_s.at[d], f_r.at[d], sib, ex)

    for d in range(1, EXP):
        give_rows(d).start()
    arr_ref[0, ex] = out[ex]
    forward(0).start()
    next_hop(2)
    for d in range(1, EXP):
        if d == EXP // 2:
            next_hop(3)
            next_down(1)
        source = lax.rem(ex + EXP - d, EXP)
        remote(out.at[ex], arr_ref.at[0, source], a_s.at[d - 1], a_r.at[d - 1], me, ex).wait_recv()
        forward(d).start()
    for d in range(EXP):
        forward(d).wait()
    next_hop(4)
    for d in range(1, EXP):
        for g in range(PG):
            share(g, d).wait_send()
        give_rows(d).wait_send()


def project(attn, w_out, residual, gain, ids, weights):
    dma = pltpu.SemaphoreType.DMA
    vmem, hbm = pl.BlockSpec(memory_space=pltpu.VMEM), pl.BlockSpec(memory_space=HBM)
    return pl.pallas_call(
        project_kernel,
        out_shape=(
            jax.ShapeDtypeStruct((NC, EXPERTS, CAP, D), BF16),
            jax.ShapeDtypeStruct((ROWS, D), BF16),
            WSHAPE,
        ),
        in_specs=[vmem, hbm, vmem, vmem, vmem, hbm],
        out_specs=(vmem, vmem, hbm),
        input_output_aliases={5: 2},
        scratch_shapes=[
            pltpu.VMEM((WL, HEADS * HD, NB), BF16),
            pltpu.VMEM((PG, EXP, ROWS, PC), BF16),
            pltpu.VMEM((PG, EXP - 1, ROWS, PC), BF16),
            pltpu.VMEM((ROWS, D), BF16),
            pltpu.VMEM((EXPERTS, CAP, D), BF16),
            dma((WL,)), dma((PG, EXP - 1)), dma((PG, EXP - 1)), dma((EXP - 1,)), dma((EXP - 1,)),
            dma((EXP,)), dma((EXP,)), dma((PROJ_HOPS, 2)), dma((PROJ_HOPS, 2)),
            dma((PROJ_DOWN, 2)), dma((PROJ_DOWN, 2)),
        ],
        compiler_params=pltpu.CompilerParams(collective_id=2, has_side_effects=True, vmem_limit_bytes=40 * MIB),
        cost_estimate=pl.CostEstimate(flops=2_200_000_000, bytes_accessed=64 * MIB, transcendentals=0),
        name="project_dispatch",
    )(attn, in_hbm(w_out), residual, gain, ids, in_hbm(weights))


SLOTS = EXPERTS * CAP
DEPTH = NC * 128
GCOLS = NC * DEPTH


def expert_kernel(
    arr_ref, w_in, hid_ref, ids_ref, gates_ref, o_ref, w_hbm,
    w, pre, act, mine, theirs, other, res, got, p_sem, d_sem, x_s, x_r, r_s, r_r, snd, rcv, d_s, d_r,
):
    me, ex, x, z, core = place()
    sib = me + 1 - 2 * core
    held = ATTN_HOPS + PROJ_HOPS + 1

    def at(step, way):
        return chip(x, z - step) if way == 0 else chip(1 - x, z + step)

    def load(kind, sem, step, way):
        c = at(step, way)
        return pltpu.make_async_copy(w_hbm.at[c, :, kind], w.at[c, :, kind], sem.at[step, way])

    for step in range(held):
        for way in range(2):
            load(PRE, p_sem, step, way).start()
    for step in range(DOWN_HELD):
        for way in range(2):
            load(DOWN, d_sem, step, way).start()
    peers = [lax.rem(ex + d, EXP) for d in range(1, EXP)]
    greet(ring_peers() + [(sib, ex)] + [(me, p) for p in peers])
    start_hop(w_hbm, PRE, held - 1, snd, rcv, 0)
    start_hop(w_hbm, DOWN, DOWN_HELD - 1, d_s, d_r, 0)
    pre[...] = jnp.zeros_like(pre)

    def use(step):
        for way in range(2):
            load(PRE, p_sem, step, way).wait()
            j = at(step, way)
            cols = pl.ds(pl.multiple_of(j * DEPTH, DEPTH), DEPTH)
            rows = arr_ref[:, :, :, cols].reshape(NC * SLOTS, DEPTH)
            tiles = [
                jnp.concatenate([w[j, c, pl.ds(t * 128, 128)] for c in range(NC)], axis=0) for t in range(2 * TILES)
            ]
            pre[...] += jnp.dot(rows, jnp.concatenate(tiles, axis=1), preferred_element_type=F32)

    def next_down(i):
        slot = i - DOWN_HELD + 1
        finish_hop(w_hbm, DOWN, i, d_s, d_r, slot)
        if i + 1 < NZ - 1:
            start_hop(w_hbm, DOWN, i + 1, d_s, d_r, slot + 1)
        for way in range(2):
            load(DOWN, d_sem, i + 1, way).start()

    @pl.loop(0, held)
    def _(step):
        use(step)

    next_down(DOWN_HELD - 1)
    for i in range(EXPERT_HOPS):
        finish_hop(w_hbm, PRE, held - 1 + i, snd, rcv, i)
        if i + 1 < EXPERT_HOPS:
            start_hop(w_hbm, PRE, held + i, snd, rcv, i + 1)
        for way in range(2):
            load(PRE, p_sem, held + i, way).start()
        use(held + i)

    gate = pre[:, :FH]
    act[...] = (gate / (1.0 + jnp.exp(-gate)) * pre[:, FH:]).astype(BF16)

    def swap(t):
        return remote(theirs.at[t], other.at[t], x_s.at[t], x_r.at[t], sib, ex)

    def give(t, d):
        p = lax.rem(ex + d, EXP)
        return remote(res.at[t, p], got.at[t, ex], r_s.at[t, d - 1], r_r.at[t, d - 1], me, p)

    def finish(t):
        swap(t).wait_recv()
        res[t] = (mine[t] + other[t]).astype(BF16).reshape(EXPERTS, CAP, GCOLS)
        for d in range(1, EXP):
            give(t, d).start()
        got[t, ex] = res[t, ex]

    first, second = slots(ids_ref)
    picks = jnp.concatenate([first, second], axis=0).astype(BF16)
    weight = [gates_ref[:, k : k + 1] for k in range(2)]

    def combine(t):
        for d in range(1, EXP):
            source = lax.rem(ex + EXP - d, EXP)
            remote(res.at[t, ex], got.at[t, source], r_s.at[t, d - 1], r_r.at[t, d - 1], me, ex).wait_recv()
        both = jnp.dot(picks, got[t].reshape(SLOTS, GCOLS), preferred_element_type=F32)
        total = weight[0] * both[:ROWS] + weight[1] * both[ROWS:]
        for way in range(2):
            cols = pl.ds(pl.multiple_of(at(t, way) * DEPTH, DEPTH), DEPTH)
            part = total[:, way * DEPTH : (way + 1) * DEPTH]
            o_ref[:, cols] = (hid_ref[:, cols].astype(F32) + part).astype(BF16)

    for t in range(NZ):
        if t in TAKEN:
            next_down(DOWN_HELD + TAKEN.index(t))
        for way in range(2):
            load(DOWN, d_sem, t, way).wait()
            down = jnp.concatenate([w[at(t, way), c, DOWN] for c in range(NC)], axis=1)
            made = jnp.dot(act[...], down, preferred_element_type=F32)
            mine[t, :, way * DEPTH : (way + 1) * DEPTH] = made[:SLOTS]
            theirs[t, :, way * DEPTH : (way + 1) * DEPTH] = made[SLOTS:]
        swap(t).start()
        if t >= 1:
            finish(t - 1)
        if t >= LAG:
            combine(t - LAG)
    finish(NZ - 1)
    for t in range(NZ - LAG, NZ):
        combine(t)
    for t in range(NZ):
        swap(t).wait_send()
        for d in range(1, EXP):
            give(t, d).wait_send()


LAG = 4
TAKEN = (1, 3, 6)


def experts(arrived, weights, hidden, ids, gates):
    vmem, hbm = pl.BlockSpec(memory_space=pltpu.VMEM), pl.BlockSpec(memory_space=HBM)
    return pl.pallas_call(
        expert_kernel,
        out_shape=(jax.ShapeDtypeStruct((ROWS, D), BF16), WSHAPE),
        in_specs=[vmem, hbm, vmem, vmem, vmem],
        out_specs=(vmem, hbm),
        input_output_aliases={1: 1},
        scratch_shapes=[
            pltpu.VMEM((CHIPS, NC, 3 * FH, 128), BF16),
            pltpu.VMEM((NC * SLOTS, 2 * FH), F32),
            pltpu.VMEM((NC * SLOTS, FH), BF16),
            pltpu.VMEM((NZ, SLOTS, GCOLS), F32),
            pltpu.VMEM((NZ, SLOTS, GCOLS), F32),
            pltpu.VMEM((NZ, SLOTS, GCOLS), F32),
            pltpu.VMEM((NZ, EXPERTS, CAP, GCOLS), BF16),
            pltpu.VMEM((NZ, EXPERTS, CAP, GCOLS), BF16),
            pltpu.SemaphoreType.DMA((NZ, 2)),
            pltpu.SemaphoreType.DMA((NZ, 2)),
            pltpu.SemaphoreType.DMA((NZ,)),
            pltpu.SemaphoreType.DMA((NZ,)),
            pltpu.SemaphoreType.DMA((NZ, EXP - 1)),
            pltpu.SemaphoreType.DMA((NZ, EXP - 1)),
            pltpu.SemaphoreType.DMA((EXPERT_HOPS, 2)),
            pltpu.SemaphoreType.DMA((EXPERT_HOPS, 2)),
            pltpu.SemaphoreType.DMA((NZ - DOWN_HELD, 2)),
            pltpu.SemaphoreType.DMA((NZ - DOWN_HELD, 2)),
        ],
        compiler_params=pltpu.CompilerParams(collective_id=3, has_side_effects=True, vmem_limit_bytes=48 * MIB),
        cost_estimate=pl.CostEstimate(flops=2_500_000_000, bytes_accessed=32 * MIB, transcendentals=100_000),
        name="experts",
    )(arrived, in_hbm(weights), hidden, ids, gates)[0]


def body(queries, keys, values, w_out, residual, norm_gain, expert_ids, gate_weights, w_gate, w_up, w_down):
    attn, weights = attention(queries, keys, values, w_gate[0], w_up[0], w_down[0])
    arrived, hidden, weights = project(attn, w_out, residual, norm_gain.reshape(1, D), expert_ids, weights)
    return experts(arrived, weights, hidden, expert_ids, gate_weights)


def solution(mesh):
    placed = (
        P("ctx", "exp"),
        P("ctx", None),
        P("ctx", None),
        P("exp", None),
        P(("ctx", "exp"), None),
        P(),
        P(("ctx", "exp"), None),
        P(("ctx", "exp"), None),
        P("exp", "ctx", None),
        P("exp", "ctx", None),
        P("exp", None, "ctx"),
    )
    return jax.shard_map(
        body, mesh=mesh, in_specs=placed, out_specs=P(("ctx", "exp"), None), check_vma=False
    )
```

time: 206 us -> 164 us (0.80)
  Pallas kernels: 192 us -> 163 us
  local copies, waits for them, and re-layouts: 13.7 us -> 0.91 us
    pallas_call x2 -> x1, Pallas kernels: 67.1 us -> 50.9 us  [attention(): pl.pallas_call(attn_kernel, out_shape=(jax.ShapeDtypeStruct((TOK, HEADS *...]
    pallas_call x1, Pallas kernels: 75.8 us -> 60 us  [project(): pl.pallas_call(project_kernel, out_shape=(jax.ShapeDtypeStruct((NC, EXPER...]
    unnamed x27 -> x11, local copies, waits for them, and re-layouts: 13.6 us -> 0.9 us
    pallas_call x1, Pallas kernels: 49.3 us -> 51.7 us  [experts(): pl.pallas_call(expert_kernel, out_shape=(jax.ShapeDtypeStruct((ROWS, D),...]
where the time goes in v2:
time: 164 us
  Pallas kernels  163 us (99%)
    pallas_call x1, Pallas kernels, project(): pl.pallas_call(project_kernel, out_shape=(jax.ShapeDtypeStruct((NC, EXPER...  60 us
    pallas_call x1, Pallas kernels, experts(): pl.pallas_call(expert_kernel, out_shape=(jax.ShapeDtypeStruct((ROWS, D),...  51.7 us
    pallas_call x1, Pallas kernels, attention(): pl.pallas_call(attn_kernel, out_shape=(jax.ShapeDtypeStruct((TOK, HEADS *...  50.9 us

profile of v2, /device:TPU:1, one launch (start us, length us, event | category | flops | bytes accessed | tf_op | source)
XLA Modules:
  0.0 163.6 jit_solution(12213294872496627441)
XLA Ops:
  0.0 0.0 copy-start.2
  0.0 0.0 copy-start.1
  0.0 0.0 copy-start
  0.0 50.9 %attention.1 = (bf16[256,1024]{1,0:T(8,128)(2,1)S(1)}, bf16[16,2,1152,128]{3,2,1,0:T(8,128)(2,1)}) custom-call(bf16[256,1024]{1,0:T(8,128)(2,1)} %q_ref.1, bf16[256,512]{1,0:T(8,128)(2,1)} %k_ref.1, bf16[256,512]{1,0:T(8,128)(2,1)} %v_ref.1, bf16[128,768]{1,0:T(8,128)(2,1)} %bitcast.3, bf16[128,768]{1,0:T(8,128)(2,1)} %bitcast.4, bf16[768,128]{1,0:T(8,128)(2,1)} %bitcast.5), custom_call_target="tpu_custom_call" | custom-call | flops 8999999488 | bytes 67108864 | tf_op jit(solution)/shard_map/attention/pallas_call | solution.py:286
  50.9 0.0 copy-start.3
  50.9 0.0 copy-done.2
  50.9 0.1 copy.14.ids_ref
  51.0 0.0 copy-done.1
  51.0 0.0 copy-done
  51.0 60.0 %project_dispatch.1 = (bf16[2,8,16,4096]{3,2,1,0:T(8,128)(2,1)S(1)}, bf16[32,4096]{1,0:T(8,128)(2,1)S(1)}, bf16[16,2,1152,128]{3,2,1,0:T(8,128)(2,1)}) custom-call(bf16[256,1024]{1,0:T(8,128)(2,1)S(1)} %get-tuple-element.11.o_ref, bf16[1024,4096]{1,0:T(8,128)(2,1)} %w_hbm.1, bf16[32,4096]{1,0:T(8,128)(2,1)S(1)} %copy-done, ...), custom_call_target="tpu_custom_call", output_to_operand_aliasing={{2}: (5, {})} | custom-call | flops 2200000000 | bytes 67108864 | tf_op jit(solution)/shard_map/project_dispatch/pallas_call | solution.py:427
  111.0 0.0 copy-done.3
  111.1 0.1 copy.16.gates_ref
  111.1 51.7 %experts.1 = (bf16[32,4096]{1,0:T(8,128)(2,1)S(1)}, bf16[16,2,1152,128]{3,2,1,0:T(8,128)(2,1)}) custom-call(bf16[2,8,16,4096]{3,2,1,0:T(8,128)(2,1)S(1)} %get-tuple-element.13.arr_ref, bf16[16,2,1152,128]{3,2,1,0:T(8,128)(2,1)} %get-tuple-element.14.w_in, bf16[32,4096]{1,0:T(8,128)(2,1)S(1)} %get-tuple-element.15.hid_ref, ...), custom_call_target="tpu_custom_call", output_to_operand_aliasing={{1}: (1, {})} | custom-call | flops 2500000000 | bytes 33554432 | tf_op jit(solution)/shard_map/experts/pallas_call | solution.py:578
  162.9 0.7 copy.20
  (1 shorter events, 0.0 us)
Async XLA Ops:
  0.0 50.9 %copy-start.2 = (s32[32,2]{0,1:T(2,128)S(1)}, s32[32,2]{0,1:T(2,128)}, u32[]{:S(2)}) copy-start(s32[32,2]{0,1:T(2,128)} %param.17) | copy-start | bytes 772
  0.0 51.0 %copy-start.1 = (bf16[4096]{0:T(1024)(128)(2,1)S(1)}, bf16[4096]{0:T(1024)(128)(2,1)}, u32[]{:S(2)}) copy-start(bf16[4096]{0:T(1024)(128)(2,1)} %param.16) | copy-start | bytes 24580
  0.0 51.0 %copy-start = (bf16[32,4096]{1,0:T(8,128)(2,1)S(1)}, bf16[32,4096]{1,0:T(8,128)(2,1)}, u32[]{:S(2)}) copy-start(bf16[32,4096]{1,0:T(8,128)(2,1)} %res_ref.1) | copy-start | bytes 786436
  50.9 60.1 %copy-start.3 = (f32[32,2]{0,1:T(2,128)S(1)}, f32[32,2]{0,1:T(2,128)}, u32[]{:S(2)}) copy-start(f32[32,2]{0,1:T(2,128)} %param.18) | copy-start | bytes 772

commit v3 on v2

--- a/solution.py
+++ b/solution.py
@@ -77,9 +77,55 @@
         c.wait_send()
 
 
+def down_piece(w_ref, xx, step, way):
+    me, ex, x, z, core = place()
+    return w_ref.at[chip(xx, z - step if way == 0 else z + step), way, DOWN]
+
+
+def down_hop(w_ref, hop, way, snd, rcv, slot):
+    me, ex, x, z, core = place()
+    ref = down_piece(w_ref, x, hop, way)
+    return remote(ref, ref, snd.at[slot, way], rcv.at[slot, way], chunk(x, z + (1 if way == 0 else -1), core), ex)
+
+
+def down_cross(w_ref, hop, way, snd, rcv, slot):
+    me, ex, x, z, core = place()
+    ref = down_piece(w_ref, x, hop + 1, way)
+    return remote(ref, ref, snd.at[slot, way], rcv.at[slot, way], chunk(1 - x, z, core), ex)
+
+
+def start_down(w_ref, hop, snd, rcv, slot):
+    for way in range(2):
+        down_hop(w_ref, hop, way, snd, rcv, slot).start()
+
+
+def pass_down(w_ref, hop, snd, rcv, c_s, c_r, slot, last):
+    me, ex, x, z, core = place()
+    for way in range(2):
+        ref = down_piece(w_ref, x, hop + 1, way)
+        remote(ref, ref, snd.at[slot, way], rcv.at[slot, way], me, ex).wait_recv()
+    if not last:
+        start_down(w_ref, hop + 1, snd, rcv, slot + 1)
+    for way in range(2):
+        down_cross(w_ref, hop, way, c_s, c_r, slot).start()
+
+
+def crossed(w_ref, hop, c_s, c_r, slot):
+    me, ex, x, z, core = place()
+    for way in range(2):
+        ref = down_piece(w_ref, 1 - x, hop + 1, way)
+        remote(ref, ref, c_s.at[slot, way], c_r.at[slot, way], me, ex).wait_recv()
+
+
+def sent_down(w_ref, hop, snd, rcv, c_s, c_r, slot):
+    for way in range(2):
+        down_hop(w_ref, hop, way, snd, rcv, slot).wait_send()
+        down_cross(w_ref, hop, way, c_s, c_r, slot).wait_send()
+
+
 def ring_peers():
     me, ex, x, z, core = place()
-    return [(chunk(x, z + 1, core), ex), (chunk(x, z - 1, core), ex)]
+    return [(chunk(x, z + 1, core), ex), (chunk(x, z - 1, core), ex), (chunk(1 - x, z, core), ex)]
 
 
 HBM = pltpu.HBM
@@ -111,7 +157,7 @@
 def attn_kernel(
     q_ref, k_ref, v_ref, g_ref, u_ref, d_ref, o_ref, w_ref,
     kv, qs, acc, m_sc, vx,
-    kv_l, q_l, own_s, own_r, ring_s, ring_r, sib_s, sib_r, w_l, w_s, w_r, wx_s, wx_r, snd, rcv, d_s, d_r,
+    kv_l, q_l, own_s, own_r, ring_s, ring_r, sib_s, sib_r, w_l, w_s, w_r, wx_s, wx_r, snd, rcv, d_s, d_r, c_s, c_r,
 ):
     me, ex, x, z, core = place()
     up, down = chunk(x, z + 1, core), chunk(x, z - 1, core)
@@ -227,7 +273,11 @@
         def _():
             wcross.wait_recv()
             start_hop(w_ref, PRE, 0, snd, rcv, 0)
-            start_hop(w_ref, DOWN, 0, d_s, d_r, 0)
+            start_down(w_ref, 0, d_s, d_r, 0)
+
+        @pl.when(u == NZ)
+        def _():
+            pass_down(w_ref, 0, d_s, d_r, c_s, c_r, 0, True)
 
         turn = u - 1
         way = lax.rem(turn + 2, 2)
@@ -268,7 +318,8 @@
             made = (acc[which, rows, :HD] / acc[which, rows, HD:]).astype(BF16)
             o_ref[pl.ds(which * HALF, HALF), pl.ds(h * HD, HD)] = made
     finish_hop(w_ref, PRE, 0, snd, rcv, 0)
-    finish_hop(w_ref, DOWN, 0, d_s, d_r, 0)
+    crossed(w_ref, 0, c_s, c_r, 0)
+    sent_down(w_ref, 0, d_s, d_r, c_s, c_r, 0)
     cross.wait_send()
     wcross.wait_send()
     for c in wsent:
@@ -299,6 +350,7 @@
             dma((2, NZ - 1)), dma((2, NZ - 1)), dma((2, NZ)), dma((2, NZ)),
             dma((NP,)), dma((NP,)), dma((NP,)), dma, dma,
             dma((ATTN_HOPS, 2)), dma((ATTN_HOPS, 2)), dma((ATTN_DOWN, 2)), dma((ATTN_DOWN, 2)),
+            dma((ATTN_DOWN, 2)), dma((ATTN_DOWN, 2)),
         ],
         compiler_params=pltpu.CompilerParams(collective_id=1, has_side_effects=True, vmem_limit_bytes=32 * MIB),
         cost_estimate=pl.CostEstimate(flops=9_000_000_000, bytes_accessed=64 * MIB, transcendentals=9_000_000),
@@ -324,7 +376,7 @@
 
 def project_kernel(
     o_ref, w_hbm, res_ref, gain_ref, ids_ref, e_in, arr_ref, hid_ref, e_ref,
-    w, part, recv, norm, out, w_sem, rs_s, rs_r, a_s, a_r, f_s, f_r, snd, rcv, d_s, d_r,
+    w, part, recv, norm, out, w_sem, rs_s, rs_r, a_s, a_r, f_s, f_r, snd, rcv, d_s, d_r, c_s, c_r,
 ):
     me, ex, x, z, core = place()
     sib = me + 1 - 2 * core
@@ -338,12 +390,10 @@
     peers = [lax.rem(ex + d, EXP) for d in range(1, EXP)]
     greet(ring_peers() + [(sib, ex)] + [(me, p) for p in peers])
     start_hop(e_ref, PRE, ATTN_HOPS, snd, rcv, 0)
-    start_hop(e_ref, DOWN, ATTN_DOWN, d_s, d_r, 0)
+    start_down(e_ref, ATTN_DOWN, d_s, d_r, 0)
 
     def next_down(i):
-        finish_hop(e_ref, DOWN, ATTN_DOWN + i, d_s, d_r, i)
-        if i + 1 < PROJ_DOWN:
-            start_hop(e_ref, DOWN, ATTN_DOWN + i + 1, d_s, d_r, i + 1)
+        pass_down(e_ref, ATTN_DOWN + i, d_s, d_r, c_s, c_r, i, i + 1 == PROJ_DOWN)
 
     def next_hop(i):
         finish_hop(e_ref, PRE, ATTN_HOPS + i, snd, rcv, i)
@@ -415,6 +465,9 @@
     for d in range(EXP):
         forward(d).wait()
     next_hop(4)
+    for i in range(PROJ_DOWN):
+        crossed(e_ref, ATTN_DOWN + i, c_s, c_r, i)
+        sent_down(e_ref, ATTN_DOWN + i, d_s, d_r, c_s, c_r, i)
     for d in range(1, EXP):
         for g in range(PG):
             share(g, d).wait_send()
@@ -442,7 +495,7 @@
             pltpu.VMEM((EXPERTS, CAP, D), BF16),
             dma((WL,)), dma((PG, EXP - 1)), dma((PG, EXP - 1)), dma((EXP - 1,)), dma((EXP - 1,)),
             dma((EXP,)), dma((EXP,)), dma((PROJ_HOPS, 2)), dma((PROJ_HOPS, 2)),
-            dma((PROJ_DOWN, 2)), dma((PROJ_DOWN, 2)),
+            dma((PROJ_DOWN, 2)), dma((PROJ_DOWN, 2)), dma((PROJ_DOWN, 2)), dma((PROJ_DOWN, 2)),
         ],
         compiler_params=pltpu.CompilerParams(collective_id=2, has_side_effects=True, vmem_limit_bytes=40 * MIB),
         cost_estimate=pl.CostEstimate(flops=2_200_000_000, bytes_accessed=64 * MIB, transcendentals=0),
@@ -457,7 +510,7 @@
 
 def expert_kernel(
     arr_ref, w_in, hid_ref, ids_ref, gates_ref, o_ref, w_hbm,
-    w, pre, act, mine, theirs, other, res, got, p_sem, d_sem, x_s, x_r, r_s, r_r, snd, rcv, d_s, d_r,
+    w, pre, act, mine, theirs, other, res, got, p_sem, d_sem, x_s, x_r, r_s, r_r, snd, rcv, d_s, d_r, c_s, c_r,
 ):
     me, ex, x, z, core = place()
     sib = me + 1 - 2 * core
@@ -466,25 +519,33 @@
     def at(step, way):
         return chip(x, z - step) if way == 0 else chip(1 - x, z + step)
 
-    def load(kind, sem, step, way):
+    def load(step, way):
         c = at(step, way)
-        return pltpu.make_async_copy(w_hbm.at[c, :, kind], w.at[c, :, kind], sem.at[step, way])
+        return pltpu.make_async_copy(w_hbm.at[c, :, PRE], w.at[c, :, PRE], p_sem.at[step, way])
+
+    def where(step, k):
+        way = k % 2
+        return chip(x if k < 2 else 1 - x, z - step if way == 0 else z + step), way
+
+    def load_down(step, k):
+        c, way = where(step, k)
+        return pltpu.make_async_copy(w_hbm.at[c, way, DOWN], w.at[c, way, DOWN], d_sem.at[step, k])
 
     for step in range(held):
         for way in range(2):
-            load(PRE, p_sem, step, way).start()
+            load(step, way).start()
     for step in range(DOWN_HELD):
-        for way in range(2):
-            load(DOWN, d_sem, step, way).start()
+        for k in range(4):
+            load_down(step, k).start()
     peers = [lax.rem(ex + d, EXP) for d in range(1, EXP)]
     greet(ring_peers() + [(sib, ex)] + [(me, p) for p in peers])
     start_hop(w_hbm, PRE, held - 1, snd, rcv, 0)
-    start_hop(w_hbm, DOWN, DOWN_HELD - 1, d_s, d_r, 0)
+    start_down(w_hbm, DOWN_HELD - 1, d_s, d_r, 0)
     pre[...] = jnp.zeros_like(pre)
 
     def use(step):
         for way in range(2):
-            load(PRE, p_sem, step, way).wait()
+            load(step, way).wait()
             j = at(step, way)
             cols = pl.ds(pl.multiple_of(j * DEPTH, DEPTH), DEPTH)
             rows = arr_ref[:, :, :, cols].reshape(NC * SLOTS, DEPTH)
@@ -494,12 +555,14 @@
             pre[...] += jnp.dot(rows, jnp.concatenate(tiles, axis=1), preferred_element_type=F32)
 
     def next_down(i):
-        slot = i - DOWN_HELD + 1
-        finish_hop(w_hbm, DOWN, i, d_s, d_r, slot)
-        if i + 1 < NZ - 1:
-            start_hop(w_hbm, DOWN, i + 1, d_s, d_r, slot + 1)
-        for way in range(2):
-            load(DOWN, d_sem, i + 1, way).start()
+        pass_down(w_hbm, i, d_s, d_r, c_s, c_r, i - DOWN_HELD + 1, i + 1 == NZ - 1)
+        for k in range(2):
+            load_down(i + 1, k).start()
+
+    def take_cross(i):
+        crossed(w_hbm, i, c_s, c_r, i - DOWN_HELD + 1)
+        for k in range(2, 4):
+            load_down(i + 1, k).start()
 
     @pl.loop(0, held)
     def _(step):
@@ -511,8 +574,11 @@
         if i + 1 < EXPERT_HOPS:
             start_hop(w_hbm, PRE, held + i, snd, rcv, i + 1)
         for way in range(2):
-            load(PRE, p_sem, held + i, way).start()
+            load(held + i, way).start()
+        if i == 0:
+            next_down(DOWN_HELD)
         use(held + i)
+    take_cross(DOWN_HELD - 1)
 
     gate = pre[:, :FH]
     act[...] = (gate / (1.0 + jnp.exp(-gate)) * pre[:, FH:]).astype(BF16)
@@ -541,20 +607,26 @@
             remote(res.at[t, ex], got.at[t, source], r_s.at[t, d - 1], r_r.at[t, d - 1], me, ex).wait_recv()
         both = jnp.dot(picks, got[t].reshape(SLOTS, GCOLS), preferred_element_type=F32)
         total = weight[0] * both[:ROWS] + weight[1] * both[ROWS:]
-        for way in range(2):
-            cols = pl.ds(pl.multiple_of(at(t, way) * DEPTH, DEPTH), DEPTH)
-            part = total[:, way * DEPTH : (way + 1) * DEPTH]
-            o_ref[:, cols] = (hid_ref[:, cols].astype(F32) + part).astype(BF16)
+        for k in range(4):
+            c, way = where(t, k)
+            cols = pl.ds(pl.multiple_of(c * DEPTH + way * 128, 128), 128)
+            o_ref[:, cols] = (hid_ref[:, cols].astype(F32) + total[:, k * 128 : (k + 1) * 128]).astype(BF16)
 
     for t in range(NZ):
-        if t in TAKEN:
-            next_down(DOWN_HELD + TAKEN.index(t))
-        for way in range(2):
-            load(DOWN, d_sem, t, way).wait()
-            down = jnp.concatenate([w[at(t, way), c, DOWN] for c in range(NC)], axis=1)
-            made = jnp.dot(act[...], down, preferred_element_type=F32)
-            mine[t, :, way * DEPTH : (way + 1) * DEPTH] = made[:SLOTS]
-            theirs[t, :, way * DEPTH : (way + 1) * DEPTH] = made[SLOTS:]
+        if t == 1:
+            next_down(DOWN_HELD + 1)
+            take_cross(DOWN_HELD)
+        if t == 3:
+            next_down(DOWN_HELD + 2)
+            take_cross(DOWN_HELD + 1)
+        if t == 5:
+            take_cross(DOWN_HELD + 2)
+        for k in range(4):
+            load_down(t, k).wait()
+        down = jnp.concatenate([w[where(t, k)[0], k % 2, DOWN] for k in range(4)], axis=1)
+        made = jnp.dot(act[...], down, preferred_element_type=F32)
+        mine[t] = made[:SLOTS]
+        theirs[t] = made[SLOTS:]
         swap(t).start()
         if t >= 1:
             finish(t - 1)
@@ -563,6 +635,8 @@
     finish(NZ - 1)
     for t in range(NZ - LAG, NZ):
         combine(t)
+    for i in range(DOWN_HELD - 1, NZ - 1):
+        sent_down(w_hbm, i, d_s, d_r, c_s, c_r, i - DOWN_HELD + 1)
     for t in range(NZ):
         swap(t).wait_send()
         for d in range(1, EXP):
@@ -570,7 +644,6 @@
 
 
 LAG = 4
-TAKEN = (1, 3, 6)
 
 
 def experts(arrived, weights, hidden, ids, gates):
@@ -591,13 +664,15 @@
             pltpu.VMEM((NZ, EXPERTS, CAP, GCOLS), BF16),
             pltpu.VMEM((NZ, EXPERTS, CAP, GCOLS), BF16),
             pltpu.SemaphoreType.DMA((NZ, 2)),
-            pltpu.SemaphoreType.DMA((NZ, 2)),
+            pltpu.SemaphoreType.DMA((NZ, 4)),
             pltpu.SemaphoreType.DMA((NZ,)),
             pltpu.SemaphoreType.DMA((NZ,)),
             pltpu.SemaphoreType.DMA((NZ, EXP - 1)),
             pltpu.SemaphoreType.DMA((NZ, EXP - 1)),
             pltpu.SemaphoreType.DMA((EXPERT_HOPS, 2)),
             pltpu.SemaphoreType.DMA((EXPERT_HOPS, 2)),
+            pltpu.SemaphoreType.DMA((NZ - DOWN_HELD, 2)),
+            pltpu.SemaphoreType.DMA((NZ - DOWN_HELD, 2)),
             pltpu.SemaphoreType.DMA((NZ - DOWN_HELD, 2)),
             pltpu.SemaphoreType.DMA((NZ - DOWN_HELD, 2)),
         ],

time: 164 us -> 169 us (1.030)
  Pallas kernels: 163 us -> 168 us
    pallas_call x1, Pallas kernels: 51.7 us -> 55.2 us  [experts(): pl.pallas_call(expert_kernel, out_shape=(jax.ShapeDtypeStruct((ROWS, D),...]
    pallas_call x1, Pallas kernels: 50.9 us -> 53.4 us  [attention(): pl.pallas_call(attn_kernel, out_shape=(jax.ShapeDtypeStruct((TOK, HEADS *...]
where the time goes in v3:
time: 169 us
  Pallas kernels  168 us (99%)
    pallas_call x1, Pallas kernels, project(): pl.pallas_call(project_kernel, out_shape=(jax.ShapeDtypeStruct((NC, EXPER...  59.4 us
    pallas_call x1, Pallas kernels, experts(): pl.pallas_call(expert_kernel, out_shape=(jax.ShapeDtypeStruct((ROWS, D),...  55.2 us
    pallas_call x1, Pallas kernels, attention(): pl.pallas_call(attn_kernel, out_shape=(jax.ShapeDtypeStruct((TOK, HEADS *...  53.4 us

profile of v3, /device:TPU:1, one launch (start us, length us, event | category | flops | bytes accessed | tf_op | source)
XLA Modules:
  0.0 168.9 jit_solution(2789234499625411940)
XLA Ops:
  0.0 0.0 copy-start.2
  0.0 0.0 copy-start.1
  0.0 0.0 copy-start
  0.0 53.4 %attention.1 = (bf16[256,1024]{1,0:T(8,128)(2,1)S(1)}, bf16[16,2,1152,128]{3,2,1,0:T(8,128)(2,1)}) custom-call(bf16[256,1024]{1,0:T(8,128)(2,1)} %q_ref.1, bf16[256,512]{1,0:T(8,128)(2,1)} %k_ref.1, bf16[256,512]{1,0:T(8,128)(2,1)} %v_ref.1, bf16[128,768]{1,0:T(8,128)(2,1)} %bitcast.3, bf16[128,768]{1,0:T(8,128)(2,1)} %bitcast.4, bf16[768,128]{1,0:T(8,128)(2,1)} %bitcast.5), custom_call_target="tpu_custom_call" | custom-call | flops 8999999488 | bytes 67108864 | tf_op jit(solution)/shard_map/attention/pallas_call | solution.py:337
  53.4 0.0 copy-start.3
  53.4 0.0 copy-done.2
  53.5 0.1 copy.14.ids_ref
  53.5 0.0 copy-done.1
  53.6 0.0 copy-done
  53.6 59.4 %project_dispatch.1 = (bf16[2,8,16,4096]{3,2,1,0:T(8,128)(2,1)S(1)}, bf16[32,4096]{1,0:T(8,128)(2,1)S(1)}, bf16[16,2,1152,128]{3,2,1,0:T(8,128)(2,1)}) custom-call(bf16[256,1024]{1,0:T(8,128)(2,1)S(1)} %get-tuple-element.11.o_ref, bf16[1024,4096]{1,0:T(8,128)(2,1)} %w_hbm.1, bf16[32,4096]{1,0:T(8,128)(2,1)S(1)} %copy-done, ...), custom_call_target="tpu_custom_call", output_to_operand_aliasing={{2}: (5, {})} | custom-call | flops 2200000000 | bytes 67108864 | tf_op jit(solution)/shard_map/project_dispatch/pallas_call | solution.py:480
  112.9 0.0 copy-done.3
  112.9 0.1 copy.16.gates_ref
  113.0 55.2 %experts.1 = (bf16[32,4096]{1,0:T(8,128)(2,1)S(1)}, bf16[16,2,1152,128]{3,2,1,0:T(8,128)(2,1)}) custom-call(bf16[2,8,16,4096]{3,2,1,0:T(8,128)(2,1)S(1)} %get-tuple-element.13.arr_ref, bf16[16,2,1152,128]{3,2,1,0:T(8,128)(2,1)} %get-tuple-element.14.w_in, bf16[32,4096]{1,0:T(8,128)(2,1)S(1)} %get-tuple-element.15.hid_ref, ...), custom_call_target="tpu_custom_call", output_to_operand_aliasing={{1}: (1, {})} | custom-call | flops 2500000000 | bytes 33554432 | tf_op jit(solution)/shard_map/experts/pallas_call | solution.py:651
  168.2 0.7 copy.20
  (1 shorter events, 0.0 us)
Async XLA Ops:
  0.0 53.4 %copy-start.2 = (s32[32,2]{0,1:T(2,128)S(1)}, s32[32,2]{0,1:T(2,128)}, u32[]{:S(2)}) copy-start(s32[32,2]{0,1:T(2,128)} %param.17) | copy-start | bytes 772
  0.0 53.5 %copy-start.1 = (bf16[4096]{0:T(1024)(128)(2,1)S(1)}, bf16[4096]{0:T(1024)(128)(2,1)}, u32[]{:S(2)}) copy-start(bf16[4096]{0:T(1024)(128)(2,1)} %param.16) | copy-start | bytes 24580
  0.0 53.6 %copy-start = (bf16[32,4096]{1,0:T(8,128)(2,1)S(1)}, bf16[32,4096]{1,0:T(8,128)(2,1)}, u32[]{:S(2)}) copy-start(bf16[32,4096]{1,0:T(8,128)(2,1)} %res_ref.1) | copy-start | bytes 786436
  53.4 59.5 %copy-start.3 = (f32[32,2]{0,1:T(2,128)S(1)}, f32[32,2]{0,1:T(2,128)}, u32[]{:S(2)}) copy-start(f32[32,2]{0,1:T(2,128)} %param.18) | copy-start | bytes 772

commit v4 on v2

--- a/solution.py
+++ b/solution.py
@@ -106,6 +106,7 @@
 QROWS = HEADS * HALF
 SCALE2 = math.log2(math.e) / math.sqrt(HD)
 NP = 2 * TILES + 1
+FAR = NZ // 2
 
 
 def attn_kernel(
@@ -147,16 +148,17 @@
     for c in kvl:
         c.wait()
 
-    def piece(way, step, cc):
-        return part(chip(x, z - step) if way == 0 else chip(1 - x, z + step), cc)
-
-    def hop(way, step):
-        ref = piece(way, step, core)
-        return remote(ref, ref, ring_s.at[way, step], ring_r.at[way, step], up if way == 0 else down, ex)
-
-    def share(way, step):
-        ref = piece(way, step, core)
-        return remote(ref, ref, sib_s.at[way, step], sib_r.at[way, step], sib, ex)
+    def piece(flow, step, cc):
+        return part(chip(x if flow in (0, 2) else 1 - x, z - step if flow in (0, 3) else z + step), cc)
+
+    def hop(flow, step):
+        ref = piece(flow, step, core)
+        target = up if flow in (0, 3) else down
+        return remote(ref, ref, ring_s.at[flow, step], ring_r.at[flow, step], target, ex)
+
+    def share(flow, step):
+        ref = piece(flow, step, core)
+        return remote(ref, ref, sib_s.at[flow, step], sib_r.at[flow, step], sib, ex)
 
     def shared(way, step):
         ref = piece(way, step, 1 - core)
@@ -166,10 +168,12 @@
     cross = remote(own, own, own_s, own_r, across, ex)
     cross.start()
     hop(0, 0).start()
+    hop(2, 0).start()
     share(0, 0).start()
     other = part(chip(1 - x, z), core)
     remote(other, other, own_s, own_r, me, ex).wait_recv()
     hop(1, 0).start()
+    hop(3, 0).start()
     share(1, 0).start()
     wsent = [remote(src, dst, w_s.at[i], w_r.at[i], sib, ex) for i, (src, dst) in enumerate(pieces(1 - core))]
     for c in wsent:
@@ -200,21 +204,25 @@
                 p.astype(BF16), vx[...], preferred_element_type=F32
             )
 
-    @pl.loop(0, NZ + 1)
+    @pl.loop(0, NZ)
     def _(u):
-        step = u + 1
-
-        @pl.when(step < NZ)
+        step = jnp.where(u == NZ - 3, FAR, u)
+
+        @pl.when(((u >= 1) & (u < FAR)) | (u == NZ - 3))
         def _():
-            for way in range(2):
-                ref = piece(way, step, core)
-                remote(ref, ref, ring_s.at[way, step - 1], ring_r.at[way, step - 1], me, ex).wait_recv()
-
-                @pl.when(step < NZ - 1)
+            for flow in (0, 2, 1, 3):
+                far = FAR - flow // 2
+
+                @pl.when(step <= far)
                 def _():
-                    hop(way, step).start()
-
-                share(way, step).start()
+                    ref = piece(flow, step, core)
+                    remote(ref, ref, ring_s.at[flow, step - 1], ring_r.at[flow, step - 1], me, ex).wait_recv()
+
+                    @pl.when(step < far)
+                    def _():
+                        hop(flow, step).start()
+
+                    share(flow, step).start()
 
         @pl.when(u == 2)
         def _():
@@ -223,44 +231,40 @@
                 wsent[i].wait_recv()
             wcross.start()
 
-        @pl.when(u == NZ - 2)
+        @pl.when(u == NZ - 3)
         def _():
             wcross.wait_recv()
             start_hop(w_ref, PRE, 0, snd, rcv, 0)
             start_hop(w_ref, DOWN, 0, d_s, d_r, 0)
 
-        turn = u - 1
-        way = lax.rem(turn + 2, 2)
-        pair = turn - way
-
-        @pl.when(turn >= 0)
-        def _():
-            mine = way == 0
-            for w in range(2):
-
-                @pl.when(way == w)
-                def _():
-                    shared(w, pair)
-                    shared(w, pair + 1)
-
-            c0 = jnp.where(mine, chip(x, z - pair), chip(1 - x, z + pair))
-            c1 = jnp.where(mine, chip(x, z - pair - 1), chip(1 - x, z + pair + 1))
-            vx[pl.ds(0, CK), :HD] = kv[c0, 1]
-            vx[pl.ds(CK, CK), :HD] = kv[c1, 1]
-
-            @pl.loop(0, 2)
-            def _(which):
-                start = me * TOK + which * HALF
-                full = jnp.maximum(c0, c1) * CK + CK - 1 <= start
-                some = jnp.minimum(c0, c1) * CK <= start
-
-                @pl.when(full)
-                def _():
-                    block(which, start, c0, c1, False)
-
-                @pl.when(some & jnp.logical_not(full))
-                def _():
-                    block(which, start, c0, c1, True)
+        away = (u + 1) // 2
+        odd = u % 2 == 1
+        c0 = chip(jnp.where(odd | (u == 0), x, 1 - x), z - away)
+        c1 = chip(jnp.where(odd & (u != NZ - 1), x, 1 - x), z + away)
+        ends = (u == 0) | (u == NZ - 1)
+        for flows, when in (((0, 1), ends), ((0, 2), odd & jnp.logical_not(ends)), ((1, 3), jnp.logical_not(odd | ends))):
+
+            @pl.when(when)
+            def _():
+                for flow in flows:
+                    shared(flow, away)
+
+        vx[pl.ds(0, CK), :HD] = kv[c0, 1]
+        vx[pl.ds(CK, CK), :HD] = kv[c1, 1]
+
+        @pl.loop(0, 2)
+        def _(which):
+            start = me * TOK + which * HALF
+            full = jnp.maximum(c0, c1) * CK + CK - 1 <= start
+            some = jnp.minimum(c0, c1) * CK <= start
+
+            @pl.when(full)
+            def _():
+                block(which, start, c0, c1, False)
+
+            @pl.when(some & jnp.logical_not(full))
+            def _():
+                block(which, start, c0, c1, True)
 
     for which in range(2):
         for h in range(HEADS):
@@ -273,11 +277,11 @@
     wcross.wait_send()
     for c in wsent:
         c.wait_send()
-    for way in range(2):
-        for step in range(NZ):
-            share(way, step).wait_send()
-            if step < NZ - 1:
-                hop(way, step).wait_send()
+    for flow in range(4):
+        for step in range(0 if flow < 2 else 1, FAR - flow // 2 + 1):
+            share(flow, step).wait_send()
+        for step in range(FAR - flow // 2):
+            hop(flow, step).wait_send()
 
 
 def attention(queries, keys, values, w_gate, w_up, w_down):
@@ -296,7 +300,7 @@
             pltpu.VMEM((KB, 2 * HD), BF16),
             dma((2,)), dma((2, HEADS)),
             dma, dma,
-            dma((2, NZ - 1)), dma((2, NZ - 1)), dma((2, NZ)), dma((2, NZ)),
+            dma((4, FAR)), dma((4, FAR)), dma((4, FAR + 1)), dma((4, FAR + 1)),
             dma((NP,)), dma((NP,)), dma((NP,)), dma, dma,
             dma((ATTN_HOPS, 2)), dma((ATTN_HOPS, 2)), dma((ATTN_DOWN, 2)), dma((ATTN_DOWN, 2)),
         ],

time: 164 us -> 164 us (level)
    pallas_call x1, Pallas kernels: 50.9 us -> 55.8 us  [attention(): pl.pallas_call(attn_kernel, out_shape=(jax.ShapeDtypeStruct((TOK, HEADS *...]
    pallas_call x1, Pallas kernels: 51.7 us -> 48.9 us  [experts(): pl.pallas_call(expert_kernel, out_shape=(jax.ShapeDtypeStruct((ROWS, D),...]
    pallas_call x1, Pallas kernels: 60 us -> 58.2 us  [project(): pl.pallas_call(project_kernel, out_shape=(jax.ShapeDtypeStruct((NC, EXPER...]
where the time goes in v4:
time: 164 us
  Pallas kernels  163 us (99%)
    pallas_call x1, Pallas kernels, project(): pl.pallas_call(project_kernel, out_shape=(jax.ShapeDtypeStruct((NC, EXPER...  58.2 us
    pallas_call x1, Pallas kernels, attention(): pl.pallas_call(attn_kernel, out_shape=(jax.ShapeDtypeStruct((TOK, HEADS *...  55.8 us
    pallas_call x1, Pallas kernels, experts(): pl.pallas_call(expert_kernel, out_shape=(jax.ShapeDtypeStruct((ROWS, D),...  48.9 us

profile of v4, /device:TPU:1, one launch (start us, length us, event | category | flops | bytes accessed | tf_op | source)
XLA Modules:
  0.0 163.9 jit_solution(13423253987867834478)
XLA Ops:
  0.0 0.0 copy-start.2
  0.0 0.0 copy-start.1
  0.0 0.0 copy-start
  0.0 55.8 %attention.1 = (bf16[256,1024]{1,0:T(8,128)(2,1)S(1)}, bf16[16,2,1152,128]{3,2,1,0:T(8,128)(2,1)}) custom-call(bf16[256,1024]{1,0:T(8,128)(2,1)} %q_ref.1, bf16[256,512]{1,0:T(8,128)(2,1)} %k_ref.1, bf16[256,512]{1,0:T(8,128)(2,1)} %v_ref.1, bf16[128,768]{1,0:T(8,128)(2,1)} %bitcast.3, bf16[128,768]{1,0:T(8,128)(2,1)} %bitcast.4, bf16[768,128]{1,0:T(8,128)(2,1)} %bitcast.5), custom_call_target="tpu_custom_call" | custom-call | flops 8999999488 | bytes 67108864 | tf_op jit(solution)/shard_map/attention/pallas_call | solution.py:290
  55.8 0.0 copy-start.3
  55.8 0.0 copy-done.2
  55.8 0.1 copy.14.ids_ref
  55.9 0.0 copy-done.1
  55.9 0.0 copy-done
  56.0 58.2 %project_dispatch.1 = (bf16[2,8,16,4096]{3,2,1,0:T(8,128)(2,1)S(1)}, bf16[32,4096]{1,0:T(8,128)(2,1)S(1)}, bf16[16,2,1152,128]{3,2,1,0:T(8,128)(2,1)}) custom-call(bf16[256,1024]{1,0:T(8,128)(2,1)S(1)} %get-tuple-element.11.o_ref, bf16[1024,4096]{1,0:T(8,128)(2,1)} %w_hbm.1, bf16[32,4096]{1,0:T(8,128)(2,1)S(1)} %copy-done, ...), custom_call_target="tpu_custom_call", output_to_operand_aliasing={{2}: (5, {})} | custom-call | flops 2200000000 | bytes 67108864 | tf_op jit(solution)/shard_map/project_dispatch/pallas_call | solution.py:431
  114.2 0.0 copy-done.3
  114.2 0.1 copy.16.gates_ref
  114.3 48.9 %experts.1 = (bf16[32,4096]{1,0:T(8,128)(2,1)S(1)}, bf16[16,2,1152,128]{3,2,1,0:T(8,128)(2,1)}) custom-call(bf16[2,8,16,4096]{3,2,1,0:T(8,128)(2,1)S(1)} %get-tuple-element.13.arr_ref, bf16[16,2,1152,128]{3,2,1,0:T(8,128)(2,1)} %get-tuple-element.14.w_in, bf16[32,4096]{1,0:T(8,128)(2,1)S(1)} %get-tuple-element.15.hid_ref, ...), custom_call_target="tpu_custom_call", output_to_operand_aliasing={{1}: (1, {})} | custom-call | flops 2500000000 | bytes 33554432 | tf_op jit(solution)/shard_map/experts/pallas_call | solution.py:582
  163.2 0.7 copy.20
  (1 shorter events, 0.0 us)
Async XLA Ops:
  0.0 55.8 %copy-start.2 = (s32[32,2]{0,1:T(2,128)S(1)}, s32[32,2]{0,1:T(2,128)}, u32[]{:S(2)}) copy-start(s32[32,2]{0,1:T(2,128)} %param.17) | copy-start | bytes 772
  0.0 55.9 %copy-start.1 = (bf16[4096]{0:T(1024)(128)(2,1)S(1)}, bf16[4096]{0:T(1024)(128)(2,1)}, u32[]{:S(2)}) copy-start(bf16[4096]{0:T(1024)(128)(2,1)} %param.16) | copy-start | bytes 24580
  0.0 55.9 %copy-start = (bf16[32,4096]{1,0:T(8,128)(2,1)S(1)}, bf16[32,4096]{1,0:T(8,128)(2,1)}, u32[]{:S(2)}) copy-start(bf16[32,4096]{1,0:T(8,128)(2,1)} %res_ref.1) | copy-start | bytes 786436
  55.8 58.4 %copy-start.3 = (f32[32,2]{0,1:T(2,128)S(1)}, f32[32,2]{0,1:T(2,128)}, u32[]{:S(2)}) copy-start(f32[32,2]{0,1:T(2,128)} %param.18) | copy-start | bytes 772

commit v5 on v4

--- a/solution.py
+++ b/solution.py
@@ -94,9 +94,8 @@
 
 
 PRE, DOWN = pl.ds(0, 2 * FH), pl.ds(2 * FH, FH)
-ATTN_HOPS, PROJ_HOPS = 1, 5
+ATTN_HOPS, PROJ_HOPS = 2, 5
 ATTN_DOWN, PROJ_DOWN = 1, 2
-EXPERT_HOPS = NZ - 1 - ATTN_HOPS - PROJ_HOPS
 DOWN_HELD = ATTN_DOWN + PROJ_DOWN + 1
 
 
@@ -224,18 +223,23 @@
 
                     share(flow, step).start()
 
-        @pl.when(u == 2)
+        @pl.when(u == 1)
         def _():
             for i in range(NP):
                 kept[i].wait()
                 wsent[i].wait_recv()
             wcross.start()
 
-        @pl.when(u == NZ - 3)
+        @pl.when(u == FAR)
         def _():
             wcross.wait_recv()
             start_hop(w_ref, PRE, 0, snd, rcv, 0)
             start_hop(w_ref, DOWN, 0, d_s, d_r, 0)
+
+        @pl.when(u == NZ - 1)
+        def _():
+            finish_hop(w_ref, PRE, 0, snd, rcv, 0)
+            start_hop(w_ref, PRE, 1, snd, rcv, 1)
 
         away = (u + 1) // 2
         odd = u % 2 == 1
@@ -271,7 +275,7 @@
             rows = pl.ds(h * HALF, HALF)
             made = (acc[which, rows, :HD] / acc[which, rows, HD:]).astype(BF16)
             o_ref[pl.ds(which * HALF, HALF), pl.ds(h * HD, HD)] = made
-    finish_hop(w_ref, PRE, 0, snd, rcv, 0)
+    finish_hop(w_ref, PRE, 1, snd, rcv, 1)
     finish_hop(w_ref, DOWN, 0, d_s, d_r, 0)
     cross.wait_send()
     wcross.wait_send()
@@ -461,11 +465,10 @@
 
 def expert_kernel(
     arr_ref, w_in, hid_ref, ids_ref, gates_ref, o_ref, w_hbm,
-    w, pre, act, mine, theirs, other, res, got, p_sem, d_sem, x_s, x_r, r_s, r_r, snd, rcv, d_s, d_r,
+    w, pre, act, mine, theirs, other, res, got, p_sem, d_sem, x_s, x_r, r_s, r_r, d_s, d_r,
 ):
     me, ex, x, z, core = place()
     sib = me + 1 - 2 * core
-    held = ATTN_HOPS + PROJ_HOPS + 1
 
     def at(step, way):
         return chip(x, z - step) if way == 0 else chip(1 - x, z + step)
@@ -474,7 +477,7 @@
         c = at(step, way)
         return pltpu.make_async_copy(w_hbm.at[c, :, kind], w.at[c, :, kind], sem.at[step, way])
 
-    for step in range(held):
+    for step in range(NZ):
         for way in range(2):
             load(PRE, p_sem, step, way).start()
     for step in range(DOWN_HELD):
@@ -482,7 +485,6 @@
             load(DOWN, d_sem, step, way).start()
     peers = [lax.rem(ex + d, EXP) for d in range(1, EXP)]
     greet(ring_peers() + [(sib, ex)] + [(me, p) for p in peers])
-    start_hop(w_hbm, PRE, held - 1, snd, rcv, 0)
     start_hop(w_hbm, DOWN, DOWN_HELD - 1, d_s, d_r, 0)
     pre[...] = jnp.zeros_like(pre)
 
@@ -505,18 +507,13 @@
         for way in range(2):
             load(DOWN, d_sem, i + 1, way).start()
 
-    @pl.loop(0, held)
-    def _(step):
-        use(step)
-
-    next_down(DOWN_HELD - 1)
-    for i in range(EXPERT_HOPS):
-        finish_hop(w_hbm, PRE, held - 1 + i, snd, rcv, i)
-        if i + 1 < EXPERT_HOPS:
-            start_hop(w_hbm, PRE, held + i, snd, rcv, i + 1)
-        for way in range(2):
-            load(PRE, p_sem, held + i, way).start()
-        use(held + i)
+    for half in range(2):
+
+        @pl.loop(half * NZ // 2, (half + 1) * NZ // 2)
+        def _(step):
+            use(step)
+
+        next_down(DOWN_HELD - 1 + half)
 
     gate = pre[:, :FH]
     act[...] = (gate / (1.0 + jnp.exp(-gate)) * pre[:, FH:]).astype(BF16)
@@ -552,7 +549,7 @@
 
     for t in range(NZ):
         if t in TAKEN:
-            next_down(DOWN_HELD + TAKEN.index(t))
+            next_down(DOWN_HELD + 1 + TAKEN.index(t))
         for way in range(2):
             load(DOWN, d_sem, t, way).wait()
             down = jnp.concatenate([w[at(t, way), c, DOWN] for c in range(NC)], axis=1)
@@ -574,7 +571,7 @@
 
 
 LAG = 4
-TAKEN = (1, 3, 6)
+TAKEN = (2, 5)
 
 
 def experts(arrived, weights, hidden, ids, gates):
@@ -600,8 +597,6 @@
             pltpu.SemaphoreType.DMA((NZ,)),
             pltpu.SemaphoreType.DMA((NZ, EXP - 1)),
             pltpu.SemaphoreType.DMA((NZ, EXP - 1)),
-            pltpu.SemaphoreType.DMA((EXPERT_HOPS, 2)),
-            pltpu.SemaphoreType.DMA((EXPERT_HOPS, 2)),
             pltpu.SemaphoreType.DMA((NZ - DOWN_HELD, 2)),
             pltpu.SemaphoreType.DMA((NZ - DOWN_HELD, 2)),
         ],

time: 164 us -> 160 us (0.976)
  Pallas kernels: 163 us -> 159 us
    pallas_call x1, Pallas kernels: 48.9 us -> 41.9 us  [experts(): pl.pallas_call(expert_kernel, out_shape=(jax.ShapeDtypeStruct((ROWS, D),...]
    pallas_call x1, Pallas kernels: 55.8 us -> 58.5 us  [attention(): pl.pallas_call(attn_kernel, out_shape=(jax.ShapeDtypeStruct((TOK, HEADS *...]
where the time goes in v5:
time: 160 us
  Pallas kernels  159 us (99%)
    pallas_call x1, Pallas kernels, attention(): pl.pallas_call(attn_kernel, out_shape=(jax.ShapeDtypeStruct((TOK, HEADS *...  58.5 us
    pallas_call x1, Pallas kernels, project(): pl.pallas_call(project_kernel, out_shape=(jax.ShapeDtypeStruct((NC, EXPER...  58.5 us
    pallas_call x1, Pallas kernels, experts(): pl.pallas_call(expert_kernel, out_shape=(jax.ShapeDtypeStruct((ROWS, D),...  41.9 us

profile of v5, /device:TPU:1, one launch (start us, length us, event | category | flops | bytes accessed | tf_op | source)
XLA Modules:
  0.0 159.9 jit_solution(10461274001051913759)
XLA Ops:
  0.0 0.0 copy-start.2
  0.0 0.0 copy-start.1
  0.0 0.0 copy-start
  0.0 58.5 %attention.1 = (bf16[256,1024]{1,0:T(8,128)(2,1)S(1)}, bf16[16,2,1152,128]{3,2,1,0:T(8,128)(2,1)}) custom-call(bf16[256,1024]{1,0:T(8,128)(2,1)} %q_ref.1, bf16[256,512]{1,0:T(8,128)(2,1)} %k_ref.1, bf16[256,512]{1,0:T(8,128)(2,1)} %v_ref.1, bf16[128,768]{1,0:T(8,128)(2,1)} %bitcast.3, bf16[128,768]{1,0:T(8,128)(2,1)} %bitcast.4, bf16[768,128]{1,0:T(8,128)(2,1)} %bitcast.5), custom_call_target="tpu_custom_call" | custom-call | flops 8999999488 | bytes 67108864 | tf_op jit(solution)/shard_map/attention/pallas_call | solution.py:294
  58.5 0.0 copy-start.3
  58.6 0.0 copy-done.2
  58.6 0.1 copy.14.ids_ref
  58.7 0.0 copy-done.1
  58.7 0.0 copy-done
  58.7 58.5 %project_dispatch.1 = (bf16[2,8,16,4096]{3,2,1,0:T(8,128)(2,1)S(1)}, bf16[32,4096]{1,0:T(8,128)(2,1)S(1)}, bf16[16,2,1152,128]{3,2,1,0:T(8,128)(2,1)}) custom-call(bf16[256,1024]{1,0:T(8,128)(2,1)S(1)} %get-tuple-element.11.o_ref, bf16[1024,4096]{1,0:T(8,128)(2,1)} %w_hbm.1, bf16[32,4096]{1,0:T(8,128)(2,1)S(1)} %copy-done, ...), custom_call_target="tpu_custom_call", output_to_operand_aliasing={{2}: (5, {})} | custom-call | flops 2200000000 | bytes 67108864 | tf_op jit(solution)/shard_map/project_dispatch/pallas_call | solution.py:435
  117.2 0.0 copy-done.3
  117.2 0.1 copy.16.gates_ref
  117.3 41.9 %experts.1 = (bf16[32,4096]{1,0:T(8,128)(2,1)S(1)}, bf16[16,2,1152,128]{3,2,1,0:T(8,128)(2,1)}) custom-call(bf16[2,8,16,4096]{3,2,1,0:T(8,128)(2,1)S(1)} %get-tuple-element.13.arr_ref, bf16[16,2,1152,128]{3,2,1,0:T(8,128)(2,1)} %get-tuple-element.14.w_in, bf16[32,4096]{1,0:T(8,128)(2,1)S(1)} %get-tuple-element.15.hid_ref, ...), custom_call_target="tpu_custom_call", output_to_operand_aliasing={{1}: (1, {})} | custom-call | flops 2500000000 | bytes 33554432 | tf_op jit(solution)/shard_map/experts/pallas_call | solution.py:579
  159.2 0.7 copy.20
  (1 shorter events, 0.0 us)
Async XLA Ops:
  0.0 58.6 %copy-start.2 = (s32[32,2]{0,1:T(2,128)S(1)}, s32[32,2]{0,1:T(2,128)}, u32[]{:S(2)}) copy-start(s32[32,2]{0,1:T(2,128)} %param.17) | copy-start | bytes 772
  0.0 58.7 %copy-start.1 = (bf16[4096]{0:T(1024)(128)(2,1)S(1)}, bf16[4096]{0:T(1024)(128)(2,1)}, u32[]{:S(2)}) copy-start(bf16[4096]{0:T(1024)(128)(2,1)} %param.16) | copy-start | bytes 24580
  0.0 58.7 %copy-start = (bf16[32,4096]{1,0:T(8,128)(2,1)S(1)}, bf16[32,4096]{1,0:T(8,128)(2,1)}, u32[]{:S(2)}) copy-start(bf16[32,4096]{1,0:T(8,128)(2,1)} %res_ref.1) | copy-start | bytes 786436
  58.5 58.6 %copy-start.3 = (f32[32,2]{0,1:T(2,128)S(1)}, f32[32,2]{0,1:T(2,128)}, u32[]{:S(2)}) copy-start(f32[32,2]{0,1:T(2,128)} %param.18) | copy-start | bytes 772

commit v6 on v5

--- a/solution.py
+++ b/solution.py
@@ -95,7 +95,7 @@
 
 PRE, DOWN = pl.ds(0, 2 * FH), pl.ds(2 * FH, FH)
 ATTN_HOPS, PROJ_HOPS = 2, 5
-ATTN_DOWN, PROJ_DOWN = 1, 2
+ATTN_DOWN, PROJ_DOWN = 1, 3
 DOWN_HELD = ATTN_DOWN + PROJ_DOWN + 1
 
 
@@ -377,10 +377,10 @@
             share(g, d).start()
 
     next_hop(0)
+    next_down(0)
     for g in range(PG):
         if g == 0:
             next_hop(1)
-            next_down(0)
         for d in range(1, EXP):
             share(g, d).wait_recv()
 
@@ -413,16 +413,17 @@
     arr_ref[0, ex] = out[ex]
     forward(0).start()
     next_hop(2)
+    next_down(1)
     for d in range(1, EXP):
         if d == EXP // 2:
             next_hop(3)
-            next_down(1)
         source = lax.rem(ex + EXP - d, EXP)
         remote(out.at[ex], arr_ref.at[0, source], a_s.at[d - 1], a_r.at[d - 1], me, ex).wait_recv()
         forward(d).start()
     for d in range(EXP):
         forward(d).wait()
     next_hop(4)
+    next_down(2)
     for d in range(1, EXP):
         for g in range(PG):
             share(g, d).wait_send()
@@ -571,7 +572,7 @@
 
 
 LAG = 4
-TAKEN = (2, 5)
+TAKEN = (2,)
 
 
 def experts(arrived, weights, hidden, ids, gates):

time: 160 us -> 161 us (level)
    pallas_call x1, Pallas kernels: 58.5 us -> 63.3 us  [project(): pl.pallas_call(project_kernel, out_shape=(jax.ShapeDtypeStruct((NC, EXPER...]
    pallas_call x1, Pallas kernels: 41.9 us -> 38.2 us  [experts(): pl.pallas_call(expert_kernel, out_shape=(jax.ShapeDtypeStruct((ROWS, D),...]
where the time goes in v6:
time: 161 us
  Pallas kernels  160 us (99%)
    pallas_call x1, Pallas kernels, project(): pl.pallas_call(project_kernel, out_shape=(jax.ShapeDtypeStruct((NC, EXPER...  63.3 us
    pallas_call x1, Pallas kernels, attention(): pl.pallas_call(attn_kernel, out_shape=(jax.ShapeDtypeStruct((TOK, HEADS *...  58.5 us
    pallas_call x1, Pallas kernels, experts(): pl.pallas_call(expert_kernel, out_shape=(jax.ShapeDtypeStruct((ROWS, D),...  38.2 us

profile of v6, /device:TPU:1, one launch (start us, length us, event | category | flops | bytes accessed | tf_op | source)
XLA Modules:
  0.0 161.0 jit_solution(8795390107300586808)
XLA Ops:
  0.0 0.0 copy-start.2
  0.0 0.0 copy-start.1
  0.0 0.0 copy-start
  0.0 58.5 %attention.1 = (bf16[256,1024]{1,0:T(8,128)(2,1)S(1)}, bf16[16,2,1152,128]{3,2,1,0:T(8,128)(2,1)}) custom-call(bf16[256,1024]{1,0:T(8,128)(2,1)} %q_ref.1, bf16[256,512]{1,0:T(8,128)(2,1)} %k_ref.1, bf16[256,512]{1,0:T(8,128)(2,1)} %v_ref.1, bf16[128,768]{1,0:T(8,128)(2,1)} %bitcast.3, bf16[128,768]{1,0:T(8,128)(2,1)} %bitcast.4, bf16[768,128]{1,0:T(8,128)(2,1)} %bitcast.5), custom_call_target="tpu_custom_call" | custom-call | flops 8999999488 | bytes 67108864 | tf_op jit(solution)/shard_map/attention/pallas_call | solution.py:294
  58.5 0.0 copy-start.3
  58.6 0.0 copy-done.2
  58.6 0.1 copy.14.ids_ref
  58.7 0.0 copy-done.1
  58.7 0.0 copy-done
  58.7 63.3 %project_dispatch.1 = (bf16[2,8,16,4096]{3,2,1,0:T(8,128)(2,1)S(1)}, bf16[32,4096]{1,0:T(8,128)(2,1)S(1)}, bf16[16,2,1152,128]{3,2,1,0:T(8,128)(2,1)}) custom-call(bf16[256,1024]{1,0:T(8,128)(2,1)S(1)} %get-tuple-element.11.o_ref, bf16[1024,4096]{1,0:T(8,128)(2,1)} %w_hbm.1, bf16[32,4096]{1,0:T(8,128)(2,1)S(1)} %copy-done, ...), custom_call_target="tpu_custom_call", output_to_operand_aliasing={{2}: (5, {})} | custom-call | flops 2200000000 | bytes 67108864 | tf_op jit(solution)/shard_map/project_dispatch/pallas_call | solution.py:436
  122.0 0.0 copy-done.3
  122.0 0.1 copy.16.gates_ref
  122.1 38.2 %experts.1 = (bf16[32,4096]{1,0:T(8,128)(2,1)S(1)}, bf16[16,2,1152,128]{3,2,1,0:T(8,128)(2,1)}) custom-call(bf16[2,8,16,4096]{3,2,1,0:T(8,128)(2,1)S(1)} %get-tuple-element.13.arr_ref, bf16[16,2,1152,128]{3,2,1,0:T(8,128)(2,1)} %get-tuple-element.14.w_in, bf16[32,4096]{1,0:T(8,128)(2,1)S(1)} %get-tuple-element.15.hid_ref, ...), custom_call_target="tpu_custom_call", output_to_operand_aliasing={{1}: (1, {})} | custom-call | flops 2500000000 | bytes 33554432 | tf_op jit(solution)/shard_map/experts/pallas_call | solution.py:580
  160.3 0.7 copy.20
  (1 shorter events, 0.0 us)
Async XLA Ops:
  0.0 58.6 %copy-start.2 = (s32[32,2]{0,1:T(2,128)S(1)}, s32[32,2]{0,1:T(2,128)}, u32[]{:S(2)}) copy-start(s32[32,2]{0,1:T(2,128)} %param.17) | copy-start | bytes 772
  0.0 58.7 %copy-start.1 = (bf16[4096]{0:T(1024)(128)(2,1)S(1)}, bf16[4096]{0:T(1024)(128)(2,1)}, u32[]{:S(2)}) copy-start(bf16[4096]{0:T(1024)(128)(2,1)} %param.16) | copy-start | bytes 24580
  0.0 58.7 %copy-start = (bf16[32,4096]{1,0:T(8,128)(2,1)S(1)}, bf16[32,4096]{1,0:T(8,128)(2,1)}, u32[]{:S(2)}) copy-start(bf16[32,4096]{1,0:T(8,128)(2,1)} %res_ref.1) | copy-start | bytes 786436
  58.5 63.5 %copy-start.3 = (f32[32,2]{0,1:T(2,128)S(1)}, f32[32,2]{0,1:T(2,128)}, u32[]{:S(2)}) copy-start(f32[32,2]{0,1:T(2,128)} %param.18) | copy-start | bytes 772
